TPU v7x, 512 devices: a whole 4x4x16 slice. The times are simulated.
512 devices in a mesh: mem: 16 (over z), lat: 32 (over x, y, core).
Axes of the slice: x: 4, y: 4, z: 16, core: 2. Of those that a mesh axis runs over, the one named last changes fastest.
Arguments:
- perturbation: bfloat16 [16, 160, 320, 128], P('mem', 'lat'), may hold values from -30 to 30
- owner_map: int32 [160], replicated, may hold values from 0 to 159, each once
- band_widths: int32 [16], replicated, may hold values from 1 to 20, 160 in all
Outputs:
- whitened: bfloat16 [16, 2, 160, 160, 128], P('mem', None, 'lat')
- inverse_root: float32 [16, 128, 128], replicated
Inputs may be any that keep to these rules, and one draw needn't show every extreme that they name: `owner_map`: each zonal wavenumber 0 to 159 stands at exactly one position. `band_widths`: the widths sum to 160; the widest band holds exactly 20 total wavenumbers.
All inputs are finite; a program needn't handle non-finite values.
Results may differ from a plain program's by a relative error of at most 0.0024.
The roundings to bfloat16 on the way count: a program that leaves them out, or rounds other values in their place, can miss the bound.
Values may be sent and summed in bfloat16 or wider, within the bound.
A program may use at most 64 MiB of HBM per device.

v0:
```python
import jax
import jax.numpy as jnp
from jax import lax
from jax.sharding import PartitionSpec as P

NLON = 320
MM = 160
LEVELS = 128
BANDS = 16
MOST = 20
NS_ITERS = 6


shrink_weight = 0.2


def colatitudes(lat_count):
    position = jnp.arange(lat_count, dtype=jnp.float32)
    colatitude = jnp.pi * (position + 0.5) / lat_count
    return (jnp.cos(colatitude), jnp.sin(colatitude))


def legendre_table(zonal_orders, total_orders, lat_count):
    cosine, sine_row = colatitudes(lat_count)
    counter = jnp.arange(1, total_orders + 1, dtype=jnp.float32)
    log_ratio = jnp.log((2.0 * counter - 1.0) / (2.0 * counter))
    log_factor = jnp.sum(
        jnp.where(counter[None, :] <= zonal_orders[:, None], log_ratio[None, :], 0.0), axis=1
    )
    log_norm = 0.5 * jnp.log((2.0 * zonal_orders + 1.0) / 2.0) + 0.5 * log_factor
    start_value = jnp.exp(log_norm[:, None] + zonal_orders[:, None] * jnp.log(sine_row)[None, :])
    weights = jnp.sqrt(jnp.pi / lat_count) * sine_row
    zonal = zonal_orders[:, None]

    def advance(state_pair, degree):
        previous, earlier = state_pair
        is_above = degree > zonal
        upper_coef = jnp.sqrt(
            jnp.maximum(4.0 * degree * degree - 1.0, 1.0)
            / jnp.where(is_above, degree * degree - zonal * zonal, 1.0)
        )
        lower_degree = degree - 1.0
        lower_coef = jnp.sqrt(
            jnp.maximum(lower_degree * lower_degree - zonal * zonal, 0.0)
            / jnp.maximum(4.0 * lower_degree * lower_degree - 1.0, 1.0)
        )
        climbed = upper_coef * (cosine[None, :] * previous - lower_coef * earlier)
        current = jnp.where(is_above, climbed, jnp.where(degree == zonal, start_value, 0.0))
        return ((current, previous), current * weights[None, :])

    zero_rows = jnp.zeros((zonal_orders.shape[0], lat_count), jnp.float32)
    unused_state, poly_table = lax.scan(
        advance, (zero_rows, zero_rows), jnp.arange(total_orders, dtype=jnp.float32), unroll=32
    )
    return poly_table


def fourier_table(orders, lon_count):
    longitude = jnp.arange(lon_count, dtype=jnp.int32)
    phases = orders[:, None] * longitude[None, :] % lon_count
    angles = phases.astype(jnp.float32) * (2.0 * jnp.pi / lon_count)
    scaling = jnp.sqrt(2.0 / lon_count)
    return jnp.stack([scaling * jnp.cos(angles), -scaling * jnp.sin(angles)])


def band_rows(band_widths):
    band_end = jnp.cumsum(band_widths)
    band_start = band_end - band_widths
    lowest = jnp.minimum(band_start, MM - MOST)
    slot_rows = lowest[:, None] + jnp.arange(MOST, dtype=jnp.int32)[None, :]
    band_keep = (slot_rows >= band_start[:, None]) & (slot_rows < band_end[:, None])
    return (band_start, band_end, slot_rows, band_keep)


def inverse_roots(gram, band_start, band_end, member_total):
    band_span = (band_end * band_end - band_start * band_start).astype(jnp.float32)
    covariance = gram / ((member_total - 1.0) * band_span)[:, None, None]
    identity = jnp.eye(LEVELS, dtype=jnp.float32)
    spread = jnp.trace(covariance, axis1=1, axis2=2) / LEVELS
    shrunk = (1.0 - shrink_weight) * covariance + shrink_weight * spread[:, None, None] * identity
    frobenius = jnp.sqrt(jnp.sum(shrunk * shrunk, axis=(1, 2)) + 1e-06)
    growing = shrunk / frobenius[:, None, None]
    inverse = jnp.broadcast_to(identity, shrunk.shape)
    for iteration in range(NS_ITERS):
        middle = 1.5 * identity - 0.5 * jnp.matmul(
            inverse, growing, precision=lax.Precision.HIGHEST
        )
        growing = jnp.matmul(growing, middle, precision=lax.Precision.HIGHEST)
        inverse = jnp.matmul(middle, inverse, precision=lax.Precision.HIGHEST)
    return inverse / jnp.sqrt(frobenius)[:, None, None]


def body(perturbation, owner_map, band_widths):
    members = perturbation.shape[0]
    lat_rows = perturbation.shape[1]
    lat_devices = lax.axis_size("lat")
    owned_count = MM // lat_devices
    wave_table = fourier_table(owner_map, NLON).astype(jnp.bfloat16)
    waves = jnp.einsum(
        "rpk,ajkl->arpjl", wave_table, perturbation, preferred_element_type=jnp.float32
    ).astype(jnp.bfloat16)
    owned_waves = lax.dynamic_slice_in_dim(
        owner_map, lax.axis_index("lat") * owned_count, owned_count, 0
    )
    poly_table = legendre_table(owned_waves.astype(jnp.float32), MM, lat_rows * lat_devices).astype(
        jnp.bfloat16
    )
    spectral = jnp.einsum(
        "nqj,arqjl->arqnl",
        poly_table,
        lax.all_to_all(waves, "lat", split_axis=2, concat_axis=3, tiled=True),
        preferred_element_type=jnp.float32,
    ).astype(jnp.bfloat16)
    band_start, band_end, slot_rows, band_keep = band_rows(band_widths)
    row_index = jnp.arange(MM, dtype=jnp.int32)
    selector = (row_index[:, None] == slot_rows.reshape(-1)[None, :]) & band_keep.reshape(-1)[
        None, :
    ]
    select_low = selector.astype(jnp.bfloat16)
    select_wide = selector.astype(jnp.float32)
    masked = jnp.einsum(
        "arqnl,ns->arqsl", spectral, select_low, preferred_element_type=jnp.float32
    ).astype(jnp.bfloat16)
    masked = masked.reshape(members, 2, owned_count, BANDS, MOST, LEVELS)
    partial_gram = jnp.einsum(
        "arqbtk,arqbtl->bkl", masked, masked, preferred_element_type=jnp.float32
    )
    member_total = members * lax.axis_size("mem")
    gram_total = lax.psum(partial_gram, ("mem", "lat"))
    inverse_root = inverse_roots(gram_total, band_start, band_end, member_total)
    root_low = inverse_root.astype(jnp.bfloat16)
    moved = jnp.einsum("arqbtk,blk->arqbtl", masked, root_low, preferred_element_type=jnp.float32)
    moved = moved.reshape(members, 2, owned_count, BANDS * MOST, LEVELS)
    whitened = jnp.einsum("arqsl,ns->arqnl", moved, select_wide, precision=lax.Precision.HIGHEST)
    return (whitened.astype(jnp.bfloat16), inverse_root)


def solution(mesh):
    in_specs = (P("mem", "lat", None, None), P(), P())
    out_specs = (P("mem", None, "lat", None, None), P())
    return jax.shard_map(body, mesh=mesh, in_specs=in_specs, out_specs=out_specs, check_vma=False)
```

profile of v0, /device:TPU:7, one launch (start us, length us, event | category | flops | bytes accessed | tf_op | source)
XLA Modules:
  0.0 1252.2 jit_solution(14990962967871219629)
XLA Ops:
  10.6 9.8 all-to-all-start
  21.3 718.0 %while.19 = (s32[]{:T(128)}, f32[5,160]{1,0:T(8,128)S(1)}, f32[5,160]{1,0:T(8,128)S(1)}, bf16[5,32,5,160]{3,2,1,0:T(8,128)(2,1)S(1)}, f32[5,32]{1,0:T(8,128)S(1)...) while((s32[]{:T(128)}, f32[5,160]{1,0:T(8,128)S(1)}, ...), condition=%wide.region_3.4_spmd.clone.clone, body=%wide.region_2.3_spmd.clone.clone.sunk | while | flops 370114 | bytes 1541077 | solution.py:52
  63.4 3.1 fusion.265
  132.7 3.2 fusion.261
  139.0 8.7 compare_bitcast_fusion.98
  147.8 3.1 fusion.264
  150.9 11.1 compare_bitcast_fusion.99
  207.0 3.1 fusion.265
  276.2 3.2 fusion.261
  282.6 8.7 compare_bitcast_fusion.98
  294.4 11.1 compare_bitcast_fusion.99
  350.5 3.1 fusion.265
  419.8 3.2 fusion.261
  426.1 8.7 compare_bitcast_fusion.98
  438.0 11.1 compare_bitcast_fusion.99
  494.1 3.1 fusion.265
  563.3 3.2 fusion.261
  569.7 8.7 compare_bitcast_fusion.98
  581.6 11.1 compare_bitcast_fusion.99
  637.6 3.1 fusion.265
  706.9 3.2 fusion.261
  713.2 8.7 compare_bitcast_fusion.98
  725.1 11.1 compare_bitcast_fusion.99
  743.1 475.8 %all-reduce.2.cloned.1.call-done = f32[16,128,128]{2,1,0:T(8,128)} async-done(((f32[16,128,128]{2,1,0:T(8,128)}), f32[16,128,128]{2,1,0:T(8,128)}) %all-reduce.2.cloned.1.call-update) | async-done | bytes 1048592 | tf_op jit(solution)/shard_map/psum | solution.py:129
  (298 shorter events, 120.9 us)
Async XLA Ops:
  7.2 2.0 copy-start
  7.2 13.4 %copy-start.3 = (s32[160]{0:T(256)S(1)}, s32[160]{0:T(256)}, u32[]{:S(2)}) copy-start(s32[160]{0:T(256)} %param.6) | copy-start | bytes 1924
  7.2 13.7 %copy-start.4 = (s32[16]{0:T(128)S(1)}, s32[16]{0:T(128)}, u32[]{:S(2)}) copy-start(s32[16]{0:T(128)} %param.7) | copy-start | bytes 196
  10.6 729.0 %all-to-all-start = ((bf16[1,2,160,5,128]{4,1,3,0,2:T(2,128)(2,1)}), bf16[1,2,160,5,128]{4,1,3,0,2:T(2,128)(2,1)S(1)}, u32[]{:S(2)}, u32[]{:S(2)}) async-start(bf16[1,2,160,5,128]{4,1,3,0,2:T(2,128)(2,1)} %copy.50), calls=%async_computation | async-start | bytes 819200 | tf_op jit(solution)/shard_map/all_to_all | solution.py:111
  20.5 1198.5 %all-reduce.2.cloned.1.call-start = ((), (), s32[]{:S(2)}) async-start(), calls=%async_computation.1 | async-start | bytes 2097152 | tf_op jit(solution)/shard_map/psum | solution.py:129
  1219.0 1.6 copy-start.1
  1241.8 1.0 copy-start.2
Sparse Core Ops, SparseCore 0:
  743.2 475.7 all-reduce.1
where the time goes:
time: 1260 us; the launch traced here: 1250 us
  loops' own time  497 us (39%)
  waiting for transfers between devices  476 us (38%)
  other arithmetic  218 us (17%)
  matrix products  25.7 us (2%)
  between operations  14.4 us (1%)
    another operation x1, loops' own time, legendre_table(): lax.scan(advance, (zero_rows, zero_rows), jnp.arange(total_orders, dtype=...  497 us
    psum x1, waiting for transfers between devices, body(): gram_total = lax.psum(partial_gram, ('mem', 'lat'))  476 us
    sqrt x35, other arithmetic, advance(): jnp.sqrt(jnp.maximum(4.0 * degree * degree - 1.0, 1.0) / jnp.where(is_abo...  99.5 us
    eq x10, other arithmetic, advance(): degree == zonal  99 us
  transfers between devices with their start and end apart: 2, of which 1 were waited for; matrix products, arithmetic and copies ran while one was open for 18% of the time, Pallas kernels for 0%

commit v1 on v0

v1 whole, which is shorter than its diff:
```python
import functools

import jax
import jax.numpy as jnp
import numpy as np
from jax import lax
from jax.experimental import pallas as pl
from jax.experimental.pallas import tpu as pltpu
from jax.sharding import PartitionSpec as P

NLAT = 160
NLON = 320
MM = 160
LEVELS = 128
BANDS = 16
MOST = 20
NS_ITERS = 6

shrink_weight = 0.2


def legendre_kernel(lat_count, zonal_ref, start_ref, cosine_ref, weight_ref, out_ref, rows_ref):
    zonal = zonal_ref[...]
    zonal_square = zonal * zonal
    lanes = start_ref.shape[1] // 128
    start = [start_ref[:, 128 * c : 128 * (c + 1)] for c in range(lanes)]
    cosine = [cosine_ref[:, 128 * c : 128 * (c + 1)] for c in range(lanes)]
    weight = [weight_ref[:, 128 * c : 128 * (c + 1)] for c in range(lanes)]

    def advance(step, carry):
        for inner in range(8):
            index = step * 8 + inner
            degree = index.astype(jnp.float32)
            is_above = degree > zonal
            is_equal = degree == zonal
            upper_coef = jnp.sqrt(
                jnp.maximum(4.0 * degree * degree - 1.0, 1.0)
                / jnp.where(is_above, degree * degree - zonal_square, 1.0)
            )
            lower = degree - 1.0
            lower_coef = jnp.sqrt(
                jnp.maximum(lower * lower - zonal_square, 0.0)
                / jnp.maximum(4.0 * lower * lower - 1.0, 1.0)
            )
            following = []
            for c in range(lanes):
                previous, earlier = carry[2 * c], carry[2 * c + 1]
                climbed = upper_coef * (cosine[c] * previous - lower_coef * earlier)
                current = jnp.where(is_above, climbed, jnp.where(is_equal, start[c], 0.0))
                rows_ref[index, :, 128 * c : 128 * (c + 1)] = current * weight[c]
                following += [current, previous]
            carry = tuple(following)
        return carry

    zero = jnp.zeros_like(zonal)
    lax.fori_loop(0, MM // 8, advance, (zero,) * (2 * lanes))
    for q in range(out_ref.shape[0]):
        out_ref[q] = rows_ref[:, q, :][:, :lat_count].astype(jnp.bfloat16)


def legendre_table(zonal_orders, lat_count):
    owned = zonal_orders.shape[0]
    rows, lanes = 8, (lat_count + 127) // 128 * 128
    colatitude = np.pi * (np.arange(lat_count) + 0.5) / lat_count
    counter = np.arange(1, MM + 1)
    log_ratio = np.log((2.0 * counter - 1.0) / (2.0 * counter)).astype(np.float32)
    log_sine = np.log(np.sin(colatitude)).astype(np.float32)

    def spread(row):
        return np.tile(np.pad(row, (0, lanes - lat_count)).astype(np.float32), (rows, 1))

    cosine = spread(np.cos(colatitude))
    weight = spread(np.sqrt(np.pi / lat_count) * np.sin(colatitude))
    log_factor = jnp.sum(
        jnp.where(counter[None, :] <= zonal_orders[:, None], log_ratio[None, :], 0.0), axis=1
    )
    log_norm = 0.5 * jnp.log((2.0 * zonal_orders + 1.0) / 2.0) + 0.5 * log_factor
    start = jnp.exp(log_norm[:, None] + zonal_orders[:, None] * log_sine[None, :])
    start = jnp.pad(start, ((0, rows - owned), (0, lanes - lat_count)))
    zonal = jnp.broadcast_to(jnp.pad(zonal_orders, (0, rows - owned))[:, None], (rows, 128))
    return pl.pallas_call(
        functools.partial(legendre_kernel, lat_count),
        out_shape=jax.ShapeDtypeStruct((owned, MM, lat_count), jnp.bfloat16),
        in_specs=[pl.BlockSpec(memory_space=pltpu.VMEM)] * 4,
        out_specs=pl.BlockSpec(memory_space=pltpu.VMEM),
        scratch_shapes=[pltpu.VMEM((MM, rows, lanes), jnp.float32)],
        cost_estimate=pl.CostEstimate(
            flops=40_000_000, bytes_accessed=20_000_000, transcendentals=1_000_000
        ),
    )(zonal, start, cosine, weight)


def fourier_table(orders, lon_count):
    phases = np.arange(MM)[:, None] * np.arange(lon_count)[None, :] % lon_count
    angles = phases * (2.0 * np.pi / lon_count)
    scaling = np.sqrt(2.0 / lon_count)
    waves = np.stack([scaling * np.cos(angles), -scaling * np.sin(angles)])
    waves = jnp.asarray(waves.astype(np.float32)).astype(jnp.bfloat16)
    pick = (orders[:, None] == jnp.arange(MM, dtype=jnp.int32)[None, :]).astype(jnp.bfloat16)
    return jnp.einsum(
        "pm,rmk->rpk", pick, waves, preferred_element_type=jnp.float32
    ).astype(jnp.bfloat16)


def band_rows(band_widths):
    band_end = jnp.cumsum(band_widths)
    band_start = band_end - band_widths
    lowest = jnp.minimum(band_start, MM - MOST)
    slot_rows = lowest[:, None] + jnp.arange(MOST, dtype=jnp.int32)[None, :]
    band_keep = (slot_rows >= band_start[:, None]) & (slot_rows < band_end[:, None])
    return (band_start, band_end, slot_rows, band_keep)


def inverse_roots(gram, band_start, band_end, member_total):
    band_span = (band_end * band_end - band_start * band_start).astype(jnp.float32)
    covariance = gram / ((member_total - 1.0) * band_span)[:, None, None]
    identity = jnp.eye(LEVELS, dtype=jnp.float32)
    spread = jnp.trace(covariance, axis1=1, axis2=2) / LEVELS
    shrunk = (1.0 - shrink_weight) * covariance + shrink_weight * spread[:, None, None] * identity
    frobenius = jnp.sqrt(jnp.sum(shrunk * shrunk, axis=(1, 2)) + 1e-06)
    growing = shrunk / frobenius[:, None, None]
    inverse = jnp.broadcast_to(identity, shrunk.shape)
    for iteration in range(NS_ITERS):
        middle = 1.5 * identity - 0.5 * jnp.matmul(
            inverse, growing, precision=lax.Precision.HIGHEST
        )
        growing = jnp.matmul(growing, middle, precision=lax.Precision.HIGHEST)
        inverse = jnp.matmul(middle, inverse, precision=lax.Precision.HIGHEST)
    return inverse / jnp.sqrt(frobenius)[:, None, None]


def reduced_band(partial_gram):
    pieces = lax.axis_size("lat")
    half = BANDS * LEVELS // pieces
    members = lax.axis_size("mem")
    thin = half // members
    chunks = lax.all_to_all(
        partial_gram.reshape(pieces, half, LEVELS), "lat", split_axis=0, concat_axis=0, tiled=True
    )
    own = jnp.sum(chunks, axis=0).reshape(members, thin, LEVELS)
    slices = lax.all_to_all(own, "mem", split_axis=0, concat_axis=0, tiled=True)
    total = jnp.sum(slices, axis=0)
    copies = jnp.broadcast_to(total[None], (members, thin, LEVELS))
    mine = lax.all_to_all(copies, "mem", split_axis=0, concat_axis=0, tiled=True)
    mine = mine.reshape(half, LEVELS)
    other = lax.ppermute(mine, "lat", [(d, d ^ 1) for d in range(pieces)])
    first = lax.axis_index("lat") % 2 == 0
    return jnp.where(
        first, jnp.concatenate([mine, other], axis=0), jnp.concatenate([other, mine], axis=0)
    )


def body(perturbation, owner_map, band_widths):
    members = perturbation.shape[0]
    lat_rows = perturbation.shape[1]
    lat_devices = lax.axis_size("lat")
    lat_index = lax.axis_index("lat")
    owned_count = MM // lat_devices
    wave_table = fourier_table(owner_map, NLON)
    waves = jnp.einsum(
        "rpk,ajkl->arpjl", wave_table, perturbation, preferred_element_type=jnp.float32
    ).astype(jnp.bfloat16)
    owned_waves = lax.dynamic_slice_in_dim(owner_map, lat_index * owned_count, owned_count, 0)
    poly_table = legendre_table(owned_waves.astype(jnp.float32), lat_rows * lat_devices)
    spectral = jnp.einsum(
        "qnj,arqjl->arqnl",
        poly_table,
        lax.all_to_all(waves, "lat", split_axis=2, concat_axis=3, tiled=True),
        preferred_element_type=jnp.float32,
    ).astype(jnp.bfloat16)
    band_start, band_end, slot_rows, band_keep = band_rows(band_widths)
    row_index = jnp.arange(MM, dtype=jnp.int32)
    selector = (row_index[:, None] == slot_rows.reshape(-1)[None, :]) & band_keep.reshape(-1)[
        None, :
    ]
    select_low = selector.astype(jnp.bfloat16)
    masked = jnp.einsum(
        "arqnl,ns->arqsl", spectral, select_low, preferred_element_type=jnp.float32
    ).astype(jnp.bfloat16)
    masked = masked.reshape(members, 2, owned_count, BANDS, MOST, LEVELS)
    partial_gram = jnp.einsum(
        "arqbtk,arqbtl->bkl", masked, masked, preferred_element_type=jnp.float32
    )
    member_total = members * lax.axis_size("mem")
    bands_here = lax.axis_size("lat") // BANDS
    band = lat_index // bands_here
    gram = reduced_band(partial_gram)
    own_start = lax.dynamic_slice_in_dim(band_start, band, 1, 0)
    own_end = lax.dynamic_slice_in_dim(band_end, band, 1, 0)
    own_root = inverse_roots(gram[None], own_start, own_end, member_total)[0]
    half = LEVELS // bands_here
    own_half = lax.dynamic_slice_in_dim(own_root, (lat_index % bands_here) * half, half, 0)
    copies = jnp.broadcast_to(own_half[None], (lat_devices, half, LEVELS))
    inverse_root = lax.all_to_all(copies, "lat", split_axis=0, concat_axis=0, tiled=True)
    inverse_root = inverse_root.reshape(BANDS, LEVELS, LEVELS)
    root_low = inverse_root.astype(jnp.bfloat16)
    moved = jnp.einsum("arqbtk,blk->arqbtl", masked, root_low, preferred_element_type=jnp.float32)
    moved = moved.astype(jnp.bfloat16).reshape(members, 2, owned_count, BANDS * MOST, LEVELS)
    whitened = jnp.einsum(
        "arqsl,ns->arqnl", moved, select_low, preferred_element_type=jnp.float32
    )
    return (whitened.astype(jnp.bfloat16), inverse_root)


def solution(mesh):
    in_specs = (P("mem", "lat", None, None), P(), P())
    out_specs = (P("mem", None, "lat", None, None), P())
    return jax.shard_map(body, mesh=mesh, in_specs=in_specs, out_specs=out_specs, check_vma=False)
```

time: 1260 us -> 126 us (0.10)
  the two profiles are of different devices: /device:TPU:7 before, /device:TPU:1 now
where the time goes in v1:
time: 126 us; the launch traced here: 125 us
  blocking collectives  79.3 us (63%)
  starting transfers between devices  14.8 us (12%)
  matrix products  9.04 us (7%)
  local copies, waits for them, and re-layouts  7.32 us (6%)
  waiting for transfers between devices  4.56 us (4%)
  between operations  4.3 us (3%)
  Pallas kernels  3.51 us (3%)
  other arithmetic  2.54 us (2%)
    all_to_all x1, blocking collectives, reduced_band(): slices = lax.all_to_all(own, 'mem', split_axis=0, concat_axis=0, tiled=True)  24.4 us
    all_to_all x1, blocking collectives, body(): lax.all_to_all(copies, 'lat', split_axis=0, concat_axis=0, tiled=True)  20.7 us
    all_to_all x1, blocking collectives, reduced_band(): lax.all_to_all(partial_gram.reshape(pieces, half, LEVELS), 'lat', split_a...  20.2 us
    all_to_all x1, blocking collectives, reduced_band(): lax.all_to_all(copies, 'mem', split_axis=0, concat_axis=0, tiled=True)  14 us
    all_to_all x1, starting transfers between devices, body(): lax.all_to_all(waves, 'lat', split_axis=2, concat_axis=3, tiled=True)  10.4 us
    all_to_all x1, waiting for transfers between devices, body(): lax.all_to_all(waves, 'lat', split_axis=2, concat_axis=3, tiled=True)  4.56 us
    ppermute x1, starting transfers between devices, reduced_band(): other = lax.ppermute(mine, 'lat', [(d, d ^ 1) for d in range(pieces)])  4.45 us
    pallas_call x1, Pallas kernels, legendre_table(): pl.pallas_call(functools.partial(legendre_kernel, lat_count), out_shape=j...  3.51 us
  transfers between devices with their start and end apart: 2, of which 1 were waited for; matrix products, arithmetic and copies ran while one was open for 3% of the time, Pallas kernels for 3%

profile of v1, /device:TPU:1, one launch (start us, length us, event | category | flops | bytes accessed | tf_op | source)
XLA Modules:
  0.0 125.4 jit_solution(5353351288186159407)
XLA Ops:
  0.6 1.0 copy-done
  1.6 1.5 %fusion.2 = bf16[1,2,160,5,128]{4,2,3,1,0:T(8,128)(2,1)S(1)} fusion(bf16[2,160,320]{2,1,0:T(8,128)(2,1)} %constant.106, bf16[1,5,320,128]{3,2,1,0:T(8,128)(2,1)S(1)} %copy-done, s32[160]{0:T(256)} %param.10), kind=kOutput, calls=%fused_computation.7 | convolution fusion | flops 164172800 | bytes 1024640 | tf_op jit(solution)/shard_map/rpk,ajkl->arpjl/dot_general | solution.py:160
  3.2 1.1 copy.63
  4.3 10.4 %all-to-all-start = ((bf16[1,2,160,5,128]{4,1,3,0,2:T(2,128)(2,1)}), bf16[1,2,160,5,128]{4,1,3,0,2:T(2,128)(2,1)S(1)}, u32[]{:S(2)}, u32[]{:S(2)}) async-start(bf16[1,2,160,5,128]{4,1,3,0,2:T(2,128)(2,1)} %copy.63), calls=%async_computation | async-start | bytes 819200 | tf_op jit(solution)/shard_map/all_to_all | solution.py:168
  15.1 0.6 pad.9.start_ref
  16.5 0.7 broadcast_in_dim.28.zonal_ref
  17.2 3.5 %shard_map.104 = bf16[5,160,160]{2,1,0:T(8,128)(2,1)} custom-call(f32[8,128]{1,0:T(8,128)} %broadcast_in_dim.28.zonal_ref, f32[8,256]{1,0:T(8,128)} %pad.9.start_ref, f32[8,256]{1,0:T(8,128)} %constant.99.clone.cosine_ref, f32[8,256]{1,0:T(8,128)} %constant.100.clone.weight_ref), custom_call_target="tpu_custom_call" | custom-call | flops 40000000 | bytes 20000000 | tf_op jit(solution)/shard_map/pallas_call | solution.py:81
  20.7 4.6 %all-to-all-done = bf16[1,2,160,5,128]{4,1,3,0,2:T(2,128)(2,1)S(1)} async-done(((bf16[1,2,160,5,128]{4,1,3,0,2:T(2,128)(2,1)}), bf16[1,2,160,5,128]{4,1,3,0,2:T(2,128)(2,1)S(1)}, u32[]{:S(2)}, u32[]{:S(2)}) %all-to-all-start) | async-done | bytes 409632 | tf_op jit(solution)/shard_map/all_to_all | solution.py:168
  25.5 1.3 %fusion.3 = bf16[2,5,160,128]{3,2,0,1:T(8,128)(2,1)S(1)} fusion(bf16[5,160,160]{2,1,0:T(8,128)(2,1)} %shard_map.104, bf16[2,5,160,128]{3,0,2,1:T(2,128)(2,1)S(1)} %bitcast.109), kind=kOutput, calls=%fused_computation.8 | convolution fusion | flops 65740800 | bytes 1075200 | tf_op jit(solution)/shard_map/qnj,arqjl->arqnl/dot_general | solution.py:165
  27.3 0.8 copy.67
  28.1 0.5 fusion.13
  28.7 20.2 %all_to_all.35 = f32[32,64,128]{2,1,0:T(8,128)S(1)} all-to-all(f32[32,64,128]{2,1,0:T(8,128)S(1)} %bitcast.110), channel_id=1, replica_groups=mesh['mem'=16,'lat'=32] {'lat'}, dimensions={0} | all-to-all | bytes 2097152 | tf_op jit(solution)/shard_map/all_to_all | solution.py:137
  49.0 24.4 %all_to_all.36 = f32[16,4,128]{2,1,0:T(4,128)S(1)} all-to-all(f32[16,4,128]{2,1,0:T(4,128)S(1)} %bitcast.112), channel_id=1, replica_groups=mesh['mem'=16,'lat'=32] {'mem'}, dimensions={0} | all-to-all | bytes 65536 | tf_op jit(solution)/shard_map/all_to_all | solution.py:141
  73.4 14.0 %all_to_all.37 = f32[16,4,128]{2,1,0:T(4,128)S(1)} all-to-all(f32[16,4,128]{2,1,0:T(4,128)S(1)} %broadcast_in_dim.34), channel_id=1, replica_groups=mesh['mem'=16,'lat'=32] {'mem'}, dimensions={0} | all-to-all | bytes 65536 | tf_op jit(solution)/shard_map/all_to_all | solution.py:144
  87.4 4.4 %collective-permute-start = (f32[64,128]{1,0:T(8,128)S(1)}, f32[64,128]{1,0:T(8,128)S(1)}, u32[]{:S(2)}, u32[]{:S(2)}) collective-permute-start(f32[64,128]{1,0:T(8,128)S(1)} %bitcast.113), channel_id=1, source_target_pairs={{0,1},{1,0},{2,3},{3,2},{4,5},{5,4},{6,7},{7,6},{8,9},{9,8},{10,11... | collective-permute-start | bytes 98312 | tf_op jit(solution)/shard_map/ppermute | solution.py:146
  91.8 0.5 fusion.46
  92.3 0.6 dynamic_slice.12
  94.9 0.6 select_reduce_fusion
  96.2 0.6 multiply_reduce_fusion
  101.2 20.7 %all_to_all.38 = f32[32,64,128]{2,1,0:T(8,128)S(1)} all-to-all(f32[32,64,128]{2,1,0:T(8,128)S(1)} %broadcast_in_dim.35), channel_id=1, replica_groups=mesh['mem'=16,'lat'=32] {'lat'}, dimensions={0} | all-to-all | bytes 2097152 | tf_op jit(solution)/shard_map/all_to_all | solution.py:194
  121.9 0.7 fusion
  122.6 0.7 copy.72
  123.2 1.1 fusion.4
  124.4 1.0 copy.91
  (52 shorter events, 5.6 us)
Async XLA Ops:
  0.6 1.0 copy-start
  3.2 11.5 %copy-start.1 = (s32[160]{0:T(256)S(1)}, s32[160]{0:T(256)}, u32[]{:S(2)}) copy-start(s32[160]{0:T(256)} %param.10) | copy-start | bytes 1924
  3.2 11.6 %copy-start.4 = (f32[160]{0:T(256)S(1)}, f32[160]{0:T(256)}, u32[]{:S(2)}) copy-start(f32[160]{0:T(256)} %constant.109) | copy-start | bytes 1924
  3.2 11.6 %copy-start.5 = (f32[160]{0:T(256)S(1)}, f32[160]{0:T(256)}, u32[]{:S(2)}) copy-start(f32[160]{0:T(256)} %constant.108) | copy-start | bytes 1924
  3.2 11.8 %copy-start.3 = (f32[160]{0:T(256)S(1)}, f32[160]{0:T(256)}, u32[]{:S(2)}) copy-start(f32[160]{0:T(256)} %constant.110) | copy-start | bytes 1924
  3.2 12.5 %copy-start.2 = (s32[16]{0:T(128)S(1)}, s32[16]{0:T(128)}, u32[]{:S(2)}) copy-start(s32[16]{0:T(128)} %param.11) | copy-start | bytes 196
  4.3 20.9 %all-to-all-start = ((bf16[1,2,160,5,128]{4,1,3,0,2:T(2,128)(2,1)}), bf16[1,2,160,5,128]{4,1,3,0,2:T(2,128)(2,1)S(1)}, u32[]{:S(2)}, u32[]{:S(2)}) async-start(bf16[1,2,160,5,128]{4,1,3,0,2:T(2,128)(2,1)} %copy.63), calls=%async_computation | async-start | bytes 819200 | tf_op jit(solution)/shard_map/all_to_all | solution.py:168
  87.4 7.5 %collective-permute-start = (f32[64,128]{1,0:T(8,128)S(1)}, f32[64,128]{1,0:T(8,128)S(1)}, u32[]{:S(2)}, u32[]{:S(2)}) collective-permute-start(f32[64,128]{1,0:T(8,128)S(1)} %bitcast.113), channel_id=1, source_target_pairs={{0,1},{1,0},{2,3},{3,2},{4,5},{5,4},{6,7},{7,6},{8,9},{9,8},{10,11... | collective-permute-start | bytes 98312 | tf_op jit(solution)/shard_map/ppermute | solution.py:146

commit v2 on v1

--- a/solution.py
+++ b/solution.py
@@ -15,6 +15,7 @@
 BANDS = 16
 MOST = 20
 NS_ITERS = 6
+CHIP_SIDE = 4
 
 shrink_weight = 0.2
 
@@ -111,43 +112,272 @@
     return (band_start, band_end, slot_rows, band_keep)
 
 
-def inverse_roots(gram, band_start, band_end, member_total):
-    band_span = (band_end * band_end - band_start * band_start).astype(jnp.float32)
-    covariance = gram / ((member_total - 1.0) * band_span)[:, None, None]
-    identity = jnp.eye(LEVELS, dtype=jnp.float32)
-    spread = jnp.trace(covariance, axis1=1, axis2=2) / LEVELS
-    shrunk = (1.0 - shrink_weight) * covariance + shrink_weight * spread[:, None, None] * identity
-    frobenius = jnp.sqrt(jnp.sum(shrunk * shrunk, axis=(1, 2)) + 1e-06)
-    growing = shrunk / frobenius[:, None, None]
-    inverse = jnp.broadcast_to(identity, shrunk.shape)
-    for iteration in range(NS_ITERS):
-        middle = 1.5 * identity - 0.5 * jnp.matmul(
-            inverse, growing, precision=lax.Precision.HIGHEST
-        )
-        growing = jnp.matmul(growing, middle, precision=lax.Precision.HIGHEST)
-        inverse = jnp.matmul(middle, inverse, precision=lax.Precision.HIGHEST)
-    return inverse / jnp.sqrt(frobenius)[:, None, None]
-
-
-def reduced_band(partial_gram):
-    pieces = lax.axis_size("lat")
-    half = BANDS * LEVELS // pieces
+def inverse_root_of(gram, denominator):
+    row = lax.broadcasted_iota(jnp.int32, (LEVELS, LEVELS), 0)
+    column = lax.broadcasted_iota(jnp.int32, (LEVELS, LEVELS), 1)
+    identity = (row == column).astype(jnp.float32)
+
+    def whole_sum(array):
+        return jnp.sum(jnp.sum(array, axis=0, keepdims=True), axis=1, keepdims=True)
+
+    def product(left, right):
+        return lax.dot(
+            left, right, precision=lax.Precision.HIGHEST, preferred_element_type=jnp.float32
+        )
+
+    covariance = gram / denominator
+    spread = whole_sum(covariance * identity) / LEVELS
+    shrunk = (1.0 - shrink_weight) * covariance + shrink_weight * spread * identity
+    frobenius = jnp.sqrt(whole_sum(shrunk * shrunk) + 1e-06)
+    growing = shrunk / frobenius
+    inverse = 1.5 * identity - 0.5 * growing
+    growing = product(growing, inverse)
+    for iteration in range(NS_ITERS - 1):
+        middle = 1.5 * identity - 0.5 * product(inverse, growing)
+        if iteration < NS_ITERS - 2:
+            growing = product(growing, middle)
+        inverse = product(middle, inverse)
+    return inverse / jnp.sqrt(frobenius)
+
+
+def band_kernel(
+    side,
+    chips,
+    members,
+    gram_ref,
+    denominator_ref,
+    out_ref,
+    pair,
+    summed,
+    got,
+    own_ref,
+    thin_got,
+    full,
+    pair_send,
+    pair_recv,
+    lat_send,
+    lat_recv,
+    thin_send,
+    thin_recv,
+    wide_send,
+    wide_recv,
+    half_send,
+    half_recv,
+    root_send,
+    root_recv,
+    pass_send,
+    pass_recv,
+):
+    lat = lax.axis_index("lat")
+    z = lax.axis_index("mem")
+    core = lax.rem(lat, 2)
+    chip = lax.div(lat, 2)
+    partner = chip * 2 + 1 - core
+    half = LEVELS // 2
+    rows = pl.ds(pl.multiple_of(core * half, half), half)
+    other_rows = pl.ds(pl.multiple_of((1 - core) * half, half), half)
+    wide = chips // side
+
+    def chip_after(d):
+        x = lax.rem(lax.div(chip, side) + lax.div(d, side), wide)
+        y = lax.rem(lax.rem(chip, side) + lax.rem(d, side), side)
+        return x * side + y
+
+    def chip_before(d):
+        x = lax.rem(lax.div(chip, side) + wide - lax.div(d, side), wide)
+        y = lax.rem(lax.rem(chip, side) + side - lax.rem(d, side), side)
+        return x * side + y
+
+    def z_after(d):
+        return lax.rem(z + d, members)
+
+    def tile_of(member):
+        return pl.multiple_of(lax.div(member, 2) * 8, 8)
+
+    def send(source, target, send_sem, recv_sem, device):
+        return pltpu.make_async_remote_copy(
+            src_ref=source,
+            dst_ref=target,
+            send_sem=send_sem,
+            recv_sem=recv_sem,
+            device_id=device,
+            device_id_type=pl.DeviceIdType.MESH,
+        )
+
+    def each(first, last, work):
+        def step(d, carry):
+            work(d)
+            return carry
+
+        lax.fori_loop(first, last, step, 0)
+
+    barrier = pltpu.get_barrier_semaphore()
+
+    def greet(device):
+        pl.semaphore_signal(
+            barrier, inc=1, device_id=device, device_id_type=pl.DeviceIdType.MESH
+        )
+
+    each(1, members, lambda d: greet({"mem": z_after(d)}))
+    each(1, chips, lambda d: greet({"lat": chip_after(d) * 2 + core}))
+    greet({"lat": partner})
+    pl.semaphore_wait(barrier, members + chips - 1)
+
+    def pair_copy(d):
+        return send(
+            gram_ref.at[chip_after(d), other_rows],
+            pair.at[d],
+            pair_send.at[d],
+            pair_recv.at[d],
+            {"lat": partner},
+        )
+
+    def lat_copy(d):
+        return send(
+            summed.at[d],
+            got.at[d],
+            lat_send.at[d],
+            lat_recv.at[d],
+            {"lat": chip_after(d) * 2 + core},
+        )
+
+    each(1, chips, lambda d: pair_copy(d).start())
+    pair_copy(0).start()
+
+    def forward(d):
+        pair_copy(d).wait_recv()
+        summed[d] = gram_ref[chip_after(d), rows, :] + pair[d]
+        lat_copy(d).start()
+
+    each(1, chips, forward)
+    pair_copy(0).wait_recv()
+    own = gram_ref[chip, rows, :] + pair[0]
+
+    def collect(d, total):
+        lat_copy(d).wait_recv()
+        return total + got[d]
+
+    own_ref[...] = lax.fori_loop(1, chips, collect, own)
+
+    def thin_copy(d):
+        return send(
+            own_ref.at[pl.ds(tile_of(z_after(d)), 8)],
+            thin_got.at[d],
+            thin_send.at[d],
+            thin_recv.at[d],
+            {"mem": z_after(d)},
+        )
+
+    each(1, members, lambda d: thin_copy(d).start())
+
+    def thin_collect(d, total):
+        thin_copy(d).wait_recv()
+        return total + thin_got[d]
+
+    tile = lax.fori_loop(1, members, thin_collect, own_ref[pl.ds(tile_of(z), 8), :])
+
+    def tile_rows(member):
+        return pl.ds(pl.multiple_of(core * half + tile_of(member), 8), 8)
+
+    full[tile_rows(z), :] = tile
+
+    def wide_copy(e, member):
+        return send(
+            full.at[tile_rows(member)],
+            full.at[tile_rows(member)],
+            wide_send.at[e],
+            wide_recv.at[e],
+            {"mem": z_after(2 * e)},
+        )
+
+    each(1, members // 2, lambda e: wide_copy(e, z).start())
+    each(
+        1, members // 2, lambda e: wide_copy(e, lax.rem(z + members - 2 * e, members)).wait_recv()
+    )
+    half_copy = send(
+        full.at[rows], full.at[rows], half_send.at[0], half_recv.at[0], {"lat": partner}
+    )
+    half_arrival = send(
+        full.at[other_rows], full.at[other_rows], half_send.at[0], half_recv.at[0], {"lat": partner}
+    )
+    half_copy.start()
+    half_arrival.wait_recv()
+
+    out_ref[chip] = inverse_root_of(full[...], denominator_ref[...])
+
+    def root_copy(d, owner):
+        return send(
+            out_ref.at[owner, rows],
+            out_ref.at[owner, rows],
+            root_send.at[d],
+            root_recv.at[d],
+            {"lat": chip_after(d) * 2 + core},
+        )
+
+    def pass_copy(d, which):
+        return send(
+            out_ref.at[chip_before(d), which],
+            out_ref.at[chip_before(d), which],
+            pass_send.at[d],
+            pass_recv.at[d],
+            {"lat": partner},
+        )
+
+    each(1, chips, lambda d: root_copy(d, chip).start())
+
+    def hand_over(d):
+        root_copy(d, chip_before(d)).wait_recv()
+        pass_copy(d, rows).start()
+
+    each(1, chips, hand_over)
+
+    def finish(d):
+        pass_copy(d, other_rows).wait_recv()
+        pass_copy(d, rows).wait_send()
+        root_copy(d, chip).wait_send()
+        lat_copy(d).wait_send()
+
+    each(1, chips, finish)
+    each(0, chips, lambda d: pair_copy(d).wait_send())
+    each(1, members, lambda d: thin_copy(d).wait_send())
+    each(1, members // 2, lambda e: wide_copy(e, z).wait_send())
+    half_copy.wait_send()
+
+
+def all_inverse_roots(partial_gram, denominator, side):
+    chips = partial_gram.shape[0]
     members = lax.axis_size("mem")
-    thin = half // members
-    chunks = lax.all_to_all(
-        partial_gram.reshape(pieces, half, LEVELS), "lat", split_axis=0, concat_axis=0, tiled=True
-    )
-    own = jnp.sum(chunks, axis=0).reshape(members, thin, LEVELS)
-    slices = lax.all_to_all(own, "mem", split_axis=0, concat_axis=0, tiled=True)
-    total = jnp.sum(slices, axis=0)
-    copies = jnp.broadcast_to(total[None], (members, thin, LEVELS))
-    mine = lax.all_to_all(copies, "mem", split_axis=0, concat_axis=0, tiled=True)
-    mine = mine.reshape(half, LEVELS)
-    other = lax.ppermute(mine, "lat", [(d, d ^ 1) for d in range(pieces)])
-    first = lax.axis_index("lat") % 2 == 0
-    return jnp.where(
-        first, jnp.concatenate([mine, other], axis=0), jnp.concatenate([other, mine], axis=0)
-    )
+    half = LEVELS // 2
+    dma = pltpu.SemaphoreType.DMA
+    return pl.pallas_call(
+        functools.partial(band_kernel, side, chips, members),
+        out_shape=jax.ShapeDtypeStruct((chips, LEVELS, LEVELS), jnp.float32),
+        in_specs=[pl.BlockSpec(memory_space=pltpu.VMEM)] * 2,
+        out_specs=pl.BlockSpec(memory_space=pltpu.VMEM),
+        scratch_shapes=[
+            pltpu.VMEM((chips, half, LEVELS), jnp.float32),
+            pltpu.VMEM((chips, half, LEVELS), jnp.float32),
+            pltpu.VMEM((chips, half, LEVELS), jnp.float32),
+            pltpu.VMEM((half, LEVELS), jnp.float32),
+            pltpu.VMEM((members, 8, LEVELS), jnp.float32),
+            pltpu.VMEM((LEVELS, LEVELS), jnp.float32),
+            dma((chips,)),
+            dma((chips,)),
+            dma((chips,)),
+            dma((chips,)),
+            dma((members,)),
+            dma((members,)),
+            dma((members // 2,)),
+            dma((members // 2,)),
+            dma((1,)),
+            dma((1,)),
+            dma((chips,)),
+            dma((chips,)),
+            dma((chips,)),
+            dma((chips,)),
+        ],
+        compiler_params=pltpu.CompilerParams(collective_id=0, has_side_effects=True),
+    )(partial_gram, denominator)
 
 
 def body(perturbation, owner_map, band_widths):
@@ -184,15 +414,11 @@
     member_total = members * lax.axis_size("mem")
     bands_here = lax.axis_size("lat") // BANDS
     band = lat_index // bands_here
-    gram = reduced_band(partial_gram)
     own_start = lax.dynamic_slice_in_dim(band_start, band, 1, 0)
     own_end = lax.dynamic_slice_in_dim(band_end, band, 1, 0)
-    own_root = inverse_roots(gram[None], own_start, own_end, member_total)[0]
-    half = LEVELS // bands_here
-    own_half = lax.dynamic_slice_in_dim(own_root, (lat_index % bands_here) * half, half, 0)
-    copies = jnp.broadcast_to(own_half[None], (lat_devices, half, LEVELS))
-    inverse_root = lax.all_to_all(copies, "lat", split_axis=0, concat_axis=0, tiled=True)
-    inverse_root = inverse_root.reshape(BANDS, LEVELS, LEVELS)
+    span = (own_end * own_end - own_start * own_start).astype(jnp.float32)
+    denominator = jnp.broadcast_to((member_total - 1.0) * span[:, None], (1, LEVELS))
+    inverse_root = all_inverse_roots(partial_gram, denominator, CHIP_SIDE)
     root_low = inverse_root.astype(jnp.bfloat16)
     moved = jnp.einsum("arqbtk,blk->arqbtl", masked, root_low, preferred_element_type=jnp.float32)
     moved = moved.astype(jnp.bfloat16).reshape(members, 2, owned_count, BANDS * MOST, LEVELS)

time: 126 us -> 93.2 us (0.74)
  blocking collectives: 79.3 us -> 0 us
  Pallas kernels: 3.51 us -> 61.3 us
  starting transfers between devices: 14.8 us -> 10.4 us
  waiting for transfers between devices: 4.56 us -> 1.47 us
  between operations: 4.3 us -> 2.72 us
  other arithmetic: 2.54 us -> 1.18 us
    all_to_all x4 -> x0, blocking collectives: 79.3 us -> none  [the longest x1 24.4 us: reduced_band(): slices = lax.all_to_all(own, 'mem', split_axis=0, concat_axis=0, tiled=True)]
    pallas_call x0 -> x1, Pallas kernels: none -> 57.8 us  [all_inverse_roots(): pl.pallas_call(functools.partial(band_kernel, side, chips, members), out_...]
    ppermute x1 -> x0, starting transfers between devices: 4.45 us -> none  [reduced_band(): other = lax.ppermute(mine, 'lat', [(d, d ^ 1) for d in range(pieces)])]
    dot_general x17 -> x0, matrix products: 3.43 us -> none  [the longest x6 1.22 us: inverse_roots(): jnp.matmul(inverse, growing, precision=lax.Precision.HIGHEST)]
    all_to_all x1, waiting for transfers between devices: 4.56 us -> 1.47 us  [body(): lax.all_to_all(waves, 'lat', split_axis=2, concat_axis=3, tiled=True)]
    reduce_sum x4 -> x0, other arithmetic: 1.34 us -> none  [the longest x1 0.62 us: inverse_roots(): spread = jnp.trace(covariance, axis1=1, axis2=2) / LEVELS]
  transfers between devices with their start and end apart: 2 -> 1, of which waited for: 1 -> 1; matrix products, arithmetic and copies ran while one was open for 3% -> 4% of each run, Pallas kernels for 3% -> 4%
where the time goes in v2:
time: 93.2 us; the launch traced here: 92.7 us
  Pallas kernels  61.3 us (66%)
  starting transfers between devices  10.4 us (11%)
  local copies, waits for them, and re-layouts  7.86 us (8%)
  matrix products  7.81 us (8%)
  between operations  2.72 us (3%)
  waiting for transfers between devices  1.47 us (2%)
  other arithmetic  1.18 us (1%)
    pallas_call x1, Pallas kernels, all_inverse_roots(): pl.pallas_call(functools.partial(band_kernel, side, chips, members), out_...  57.8 us
    all_to_all x1, starting transfers between devices, body(): lax.all_to_all(waves, 'lat', split_axis=2, concat_axis=3, tiled=True)  10.4 us
    pallas_call x1, Pallas kernels, legendre_table(): pl.pallas_call(functools.partial(legendre_kernel, lat_count), out_shape=j...  3.51 us
    unnamed x15, local copies, waits for them, and re-layouts  2.08 us
    dot_general x1, matrix products, body(): jnp.einsum('arqbtk,blk->arqbtl', masked, root_low, preferred_element_type...  1.91 us
  transfers between devices with their start and end apart: 1, of which 1 were waited for; matrix products, arithmetic and copies ran while one was open for 4% of the time, Pallas kernels for 4%

profile of v2, /device:TPU:1, one launch (start us, length us, event | category | flops | bytes accessed | tf_op | source)
XLA Modules:
  0.0 92.7 jit_solution(10584039889789107839)
XLA Ops:
  0.6 1.0 %copy-done = bf16[1,5,320,128]{3,2,1,0:T(8,128)(2,1)S(1)} copy-done((bf16[1,5,320,128]{3,2,1,0:T(8,128)(2,1)S(1)}, bf16[1,5,320,128]{3,2,1,0:T(8,128)(2,1)}, u32[]{:S(2)}) %copy-start) | copy-done | bytes 409624
  1.6 1.5 %fusion.2 = bf16[1,2,160,5,128]{4,2,3,1,0:T(8,128)(2,1)S(1)} fusion(bf16[2,160,320]{2,1,0:T(8,128)(2,1)} %constant.67, bf16[1,5,320,128]{3,2,1,0:T(8,128)(2,1)S(1)} %copy-done, s32[160]{0:T(256)} %param.10), kind=kOutput, calls=%fused_computation.8 | convolution fusion | flops 164172800 | bytes 1024640 | tf_op jit(solution)/shard_map/rpk,ajkl->arpjl/dot_general | solution.py:390
  3.2 1.1 %copy.41 = bf16[1,2,160,5,128]{4,1,3,0,2:T(2,128)(2,1)} copy(bf16[1,2,160,5,128]{4,2,3,1,0:T(8,128)(2,1)S(1)} %fusion.2) | data formatting | bytes 819200 | tf_op jit(solution)/shard_map/convert_element_type | solution.py:392
  4.3 10.4 %all-to-all-start = ((bf16[1,2,160,5,128]{4,1,3,0,2:T(2,128)(2,1)}), bf16[1,2,160,5,128]{4,1,3,0,2:T(2,128)(2,1)S(1)}, u32[]{:S(2)}, u32[]{:S(2)}) async-start(bf16[1,2,160,5,128]{4,1,3,0,2:T(2,128)(2,1)} %copy.41), calls=%async_computation | async-start | bytes 819200 | tf_op jit(solution)/shard_map/all_to_all | solution.py:398
  14.8 0.2 select_reduce_fusion
  15.2 0.6 pad.9.start_ref
  15.9 0.1 reduce
  16.0 0.5 fusion.28
  16.5 0.6 dynamic_slice.11
  19.3 0.1 lt.22
  19.6 0.7 broadcast_in_dim.25.zonal_ref
  20.3 3.5 %shard_map.104 = bf16[5,160,160]{2,1,0:T(8,128)(2,1)} custom-call(f32[8,128]{1,0:T(8,128)} %broadcast_in_dim.25.zonal_ref, f32[8,256]{1,0:T(8,128)} %pad.9.start_ref, f32[8,256]{1,0:T(8,128)} %constant.60.clone.cosine_ref, f32[8,256]{1,0:T(8,128)} %constant.61.clone.weight_ref), custom_call_target="tpu_custom_call" | custom-call | flops 40000000 | bytes 20000000 | tf_op jit(solution)/shard_map/pallas_call | solution.py:82
  23.8 1.5 %all-to-all-done = bf16[1,2,160,5,128]{4,1,3,0,2:T(2,128)(2,1)S(1)} async-done(((bf16[1,2,160,5,128]{4,1,3,0,2:T(2,128)(2,1)}), bf16[1,2,160,5,128]{4,1,3,0,2:T(2,128)(2,1)S(1)}, u32[]{:S(2)}, u32[]{:S(2)}) %all-to-all-start) | async-done | bytes 409632 | tf_op jit(solution)/shard_map/all_to_all | solution.py:398
  25.3 0.3 copy.42
  25.5 1.3 %fusion.3 = bf16[2,5,160,128]{3,2,0,1:T(8,128)(2,1)S(1)} fusion(bf16[5,160,160]{2,1,0:T(8,128)(2,1)} %shard_map.104, bf16[2,5,160,128]{3,0,2,1:T(2,128)(2,1)S(1)} %bitcast.73), kind=kOutput, calls=%fused_computation.9 | convolution fusion | flops 65740800 | bytes 1075200 | tf_op jit(solution)/shard_map/qnj,arqjl->arqnl/dot_general | solution.py:395
  26.8 0.5 fusion.1
  27.3 0.8 copy.45
  28.1 1.5 %convolution_bitcast_fusion.gram_ref = f32[16,128,128]{2,1,0:T(8,128)} fusion(bf16[2,5,16,20,128]{4,0,3,2,1:T(2,128)(2,1)S(1)} %bitcast.70), kind=kOutput, calls=%fused_computation.2 | convolution fusion | flops 104857600 | bytes 1867776 | tf_op jit(solution)/shard_map/arqbtk,arqbtl->bkl/dot_general | solution.py:411
  29.6 0.5 broadcast_in_dim.48.denominator_ref
  30.1 57.8 %shard_map.105 = f32[16,128,128]{2,1,0:T(8,128)} custom-call(f32[16,128,128]{2,1,0:T(8,128)} %convolution_bitcast_fusion.gram_ref, f32[1,128]{1,0:T(1,128)} %broadcast_in_dim.48.denominator_ref), custom_call_target="tpu_custom_call" | custom-call | tf_op jit(solution)/shard_map/pallas_call | solution.py:352
  88.0 1.9 %fusion = bf16[1,2,5,16,20,128]{5,4,2,1,3,0:T(8,128)(2,1)S(1)} fusion(bf16[2,5,16,20,128]{4,0,3,2,1:T(2,128)(2,1)S(1)} %bitcast.71, f32[16,128,128]{2,1,0:T(8,128)} %shard_map.105), kind=kOutput, calls=%fused_computation.3 | convolution fusion | flops 105529344 | bytes 2686976 | tf_op jit(solution)/shard_map/arqbtk,blk->arqbtl/dot_general | solution.py:423
  89.9 0.7 copy.49
  90.6 1.1 %fusion.4 = bf16[1,2,5,160,128]{4,3,2,1,0:T(8,128)(2,1)} fusion(bf16[2,5,320,128]{3,0,2,1:T(2,128)(2,1)S(1)} %bitcast.74, s32[320]{0:T(512)S(1)} %add.53, pred[320]{0:T(512)(128)(4,1)S(1)} %compare_and_fusion), kind=kOutput, calls=%fused_computation.10 | convolution fusion | flops 131379200 | bytes 1230400 | tf_op jit(solution)/shard_map/arqsl,ns->arqnl/dot_general | solution.py:425
  91.8 1.0 %copy.67 = f32[16,128,128]{2,1,0:T(8,128)} copy(f32[16,128,128]{2,1,0:T(8,128)S(1)} %copy-done.1) | data formatting | bytes 2097152
  (26 shorter events, 0.9 us)
Async XLA Ops:
  0.6 1.0 %copy-start = (bf16[1,5,320,128]{3,2,1,0:T(8,128)(2,1)S(1)}, bf16[1,5,320,128]{3,2,1,0:T(8,128)(2,1)}, u32[]{:S(2)}) copy-start(bf16[1,5,320,128]{3,2,1,0:T(8,128)(2,1)} %param.9) | copy-start | bytes 1228804
  3.2 11.5 %copy-start.2 = (s32[160]{0:T(256)S(1)}, s32[160]{0:T(256)}, u32[]{:S(2)}) copy-start(s32[160]{0:T(256)} %param.10) | copy-start | bytes 1924
  3.2 11.6 %copy-start.5 = (f32[160]{0:T(256)S(1)}, f32[160]{0:T(256)}, u32[]{:S(2)}) copy-start(f32[160]{0:T(256)} %constant.70) | copy-start | bytes 1924
  3.2 11.6 %copy-start.6 = (f32[160]{0:T(256)S(1)}, f32[160]{0:T(256)}, u32[]{:S(2)}) copy-start(f32[160]{0:T(256)} %constant.69) | copy-start | bytes 1924
  3.2 11.9 %copy-start.4 = (f32[160]{0:T(256)S(1)}, f32[160]{0:T(256)}, u32[]{:S(2)}) copy-start(f32[160]{0:T(256)} %constant.71) | copy-start | bytes 1924
  3.2 12.5 %copy-start.3 = (s32[16]{0:T(128)S(1)}, s32[16]{0:T(128)}, u32[]{:S(2)}) copy-start(s32[16]{0:T(128)} %param.11) | copy-start | bytes 196
  4.3 20.9 %all-to-all-start = ((bf16[1,2,160,5,128]{4,1,3,0,2:T(2,128)(2,1)}), bf16[1,2,160,5,128]{4,1,3,0,2:T(2,128)(2,1)S(1)}, u32[]{:S(2)}, u32[]{:S(2)}) async-start(bf16[1,2,160,5,128]{4,1,3,0,2:T(2,128)(2,1)} %copy.41), calls=%async_computation | async-start | bytes 819200 | tf_op jit(solution)/shard_map/all_to_all | solution.py:398
  90.5 1.2 %copy-start.1 = (f32[16,128,128]{2,1,0:T(8,128)S(1)}, f32[16,128,128]{2,1,0:T(8,128)}, u32[]{:S(2)}) copy-start(f32[16,128,128]{2,1,0:T(8,128)} %shard_map.105) | copy-start | bytes 3145732

commit v3 on v2

--- a/solution.py
+++ b/solution.py
@@ -13,14 +13,14 @@
 MM = 160
 LEVELS = 128
 BANDS = 16
-MOST = 20
 NS_ITERS = 6
 CHIP_SIDE = 4
+SLOTS = 32
 
 shrink_weight = 0.2
 
 
-def legendre_kernel(lat_count, zonal_ref, start_ref, cosine_ref, weight_ref, out_ref, rows_ref):
+def legendre_rows(zonal_ref, start_ref, cosine_ref, weight_ref, rows_ref):
     zonal = zonal_ref[...]
     zonal_square = zonal * zonal
     lanes = start_ref.shape[1] // 128
@@ -55,14 +55,14 @@
 
     zero = jnp.zeros_like(zonal)
     lax.fori_loop(0, MM // 8, advance, (zero,) * (2 * lanes))
-    for q in range(out_ref.shape[0]):
-        out_ref[q] = rows_ref[:, q, :][:, :lat_count].astype(jnp.bfloat16)
-
-
-def legendre_table(zonal_orders, lat_count):
+
+
+def legendre_start(zonal_orders, lat_count, lat_rows):
     owned = zonal_orders.shape[0]
     rows, lanes = 8, (lat_count + 127) // 128 * 128
-    colatitude = np.pi * (np.arange(lat_count) + 0.5) / lat_count
+    devices = lat_count // lat_rows
+    place = np.arange(lat_count)
+    colatitude = np.pi * (place % devices * lat_rows + place // devices + 0.5) / lat_count
     counter = np.arange(1, MM + 1)
     log_ratio = np.log((2.0 * counter - 1.0) / (2.0 * counter)).astype(np.float32)
     log_sine = np.log(np.sin(colatitude)).astype(np.float32)
@@ -79,16 +79,7 @@
     start = jnp.exp(log_norm[:, None] + zonal_orders[:, None] * log_sine[None, :])
     start = jnp.pad(start, ((0, rows - owned), (0, lanes - lat_count)))
     zonal = jnp.broadcast_to(jnp.pad(zonal_orders, (0, rows - owned))[:, None], (rows, 128))
-    return pl.pallas_call(
-        functools.partial(legendre_kernel, lat_count),
-        out_shape=jax.ShapeDtypeStruct((owned, MM, lat_count), jnp.bfloat16),
-        in_specs=[pl.BlockSpec(memory_space=pltpu.VMEM)] * 4,
-        out_specs=pl.BlockSpec(memory_space=pltpu.VMEM),
-        scratch_shapes=[pltpu.VMEM((MM, rows, lanes), jnp.float32)],
-        cost_estimate=pl.CostEstimate(
-            flops=40_000_000, bytes_accessed=20_000_000, transcendentals=1_000_000
-        ),
-    )(zonal, start, cosine, weight)
+    return (zonal, start, cosine, weight)
 
 
 def fourier_table(orders, lon_count):
@@ -101,15 +92,6 @@
     return jnp.einsum(
         "pm,rmk->rpk", pick, waves, preferred_element_type=jnp.float32
     ).astype(jnp.bfloat16)
-
-
-def band_rows(band_widths):
-    band_end = jnp.cumsum(band_widths)
-    band_start = band_end - band_widths
-    lowest = jnp.minimum(band_start, MM - MOST)
-    slot_rows = lowest[:, None] + jnp.arange(MOST, dtype=jnp.int32)[None, :]
-    band_keep = (slot_rows >= band_start[:, None]) & (slot_rows < band_end[:, None])
-    return (band_start, band_end, slot_rows, band_keep)
 
 
 def inverse_root_of(gram, denominator):
@@ -144,15 +126,30 @@
     side,
     chips,
     members,
+    waves_ref,
+    zonal_ref,
+    start_ref,
+    cosine_ref,
+    weight_ref,
+    select_ref,
+    spread_ref,
+    denominator_ref,
+    white_ref,
+    out_ref,
+    rows_ref,
+    arrived,
+    grid,
+    masked,
+    moved,
     gram_ref,
-    denominator_ref,
-    out_ref,
     pair,
     summed,
     got,
     own_ref,
     thin_got,
     full,
+    wave_send,
+    wave_recv,
     pair_send,
     pair_recv,
     lat_send,
@@ -188,6 +185,12 @@
         y = lax.rem(lax.rem(chip, side) + side - lax.rem(d, side), side)
         return x * side + y
 
+    def lat_after(d):
+        return chip_after(lax.div(d, 2)) * 2 + lax.rem(core + lax.rem(d, 2), 2)
+
+    def lat_before(d):
+        return chip_before(lax.div(d, 2)) * 2 + lax.rem(core + lax.rem(d, 2), 2)
+
     def z_after(d):
         return lax.rem(z + d, members)
 
@@ -219,9 +222,77 @@
         )
 
     each(1, members, lambda d: greet({"mem": z_after(d)}))
-    each(1, chips, lambda d: greet({"lat": chip_after(d) * 2 + core}))
-    greet({"lat": partner})
-    pl.semaphore_wait(barrier, members + chips - 1)
+    each(1, 2 * chips, lambda d: greet({"lat": lat_after(d)}))
+    legendre_rows(zonal_ref, start_ref, cosine_ref, weight_ref, rows_ref)
+    pl.semaphore_wait(barrier, members - 1 + 2 * chips - 1)
+
+    def wave_copy(d, source):
+        return send(
+            waves_ref.at[lat_after(d)],
+            arrived.at[source],
+            wave_send.at[d],
+            wave_recv.at[d],
+            {"lat": lat_after(d)},
+        )
+
+    each(1, 2 * chips, lambda d: wave_copy(d, lat).start())
+    arrived[lat] = waves_ref[lat]
+    each(1, 2 * chips, lambda d: wave_copy(d, lat_before(d)).wait_recv())
+    devices, per_device = arrived.shape[0], arrived.shape[1]
+    owned = masked.shape[0]
+    lat_rows = per_device // (2 * owned)
+    stride = grid.shape[0] // (devices + 1)
+    for device in range(devices):
+        grid[device * stride : device * stride + per_device] = arrived[device].astype(jnp.float32)
+
+    def field(r, q):
+        first = (r * owned + q) * lat_rows
+        parts = [grid[pl.ds(first + k, devices, stride=stride), :] for k in range(lat_rows)]
+        return jnp.concatenate(parts, axis=0)
+
+    for q in range(owned):
+        table = rows_ref[:, q, :][:, : devices * lat_rows].astype(jnp.bfloat16)
+        both = jnp.concatenate([field(0, q), field(1, q)], axis=1).astype(jnp.bfloat16)
+        coefficients = jnp.dot(table, both, preferred_element_type=jnp.float32)
+        masked[q] = jnp.dot(
+            select_ref[...],
+            coefficients.astype(jnp.bfloat16),
+            preferred_element_type=jnp.float32,
+        ).astype(jnp.bfloat16)
+
+    def band_slots(band):
+        return pl.ds(pl.multiple_of(band * SLOTS, SLOTS), SLOTS)
+
+    def band_values(band):
+        slots = band_slots(band)
+        return jnp.concatenate(
+            [
+                masked[q, slots, LEVELS * r : LEVELS * (r + 1)]
+                for q in range(owned)
+                for r in range(2)
+            ],
+            axis=0,
+        )
+
+    def add_up(band):
+        values = band_values(band)
+        gram_ref[band] = lax.dot_general(
+            values, values, (((0,), (0,)), ((), ())), preferred_element_type=jnp.float32
+        )
+
+    def whiten(band):
+        root_low = out_ref[band].astype(jnp.bfloat16)
+        turned = lax.dot_general(
+            band_values(band),
+            root_low,
+            (((1,), (1,)), ((), ())),
+            preferred_element_type=jnp.float32,
+        ).astype(jnp.bfloat16)
+        slots = band_slots(band)
+        for q in range(owned):
+            for r in range(2):
+                row = (2 * q + r) * SLOTS
+                moved[q, slots, LEVELS * r : LEVELS * (r + 1)] = turned[row : row + SLOTS]
 
     def pair_copy(d):
         return send(
@@ -241,8 +312,12 @@
             {"lat": chip_after(d) * 2 + core},
         )
 
-    each(1, chips, lambda d: pair_copy(d).start())
-    pair_copy(0).start()
+    def begin(d):
+        add_up(chip_after(d))
+        pair_copy(d).start()
+
+    each(1, chips, begin)
+    begin(0)
 
     def forward(d):
         pair_copy(d).wait_recv()
@@ -325,107 +400,110 @@
 
     each(1, chips, lambda d: root_copy(d, chip).start())
 
+    whiten(chip)
+
     def hand_over(d):
         root_copy(d, chip_before(d)).wait_recv()
         pass_copy(d, rows).start()
 
-    each(1, chips, hand_over)
+    def take_over(d):
+        pass_copy(d, other_rows).wait_recv()
+        whiten(chip_before(d))
+
+    def both_ways(d):
+        hand_over(d)
+        take_over(d - 1)
+
+    hand_over(1)
+    each(2, chips, both_ways)
+    take_over(chips - 1)
+    for q in range(owned):
+        result = jnp.dot(
+            spread_ref[...], moved[q], preferred_element_type=jnp.float32
+        ).astype(jnp.bfloat16)
+        for r in range(2):
+            white_ref[r, q] = result[:, LEVELS * r : LEVELS * (r + 1)]
 
     def finish(d):
-        pass_copy(d, other_rows).wait_recv()
         pass_copy(d, rows).wait_send()
         root_copy(d, chip).wait_send()
         lat_copy(d).wait_send()
 
     each(1, chips, finish)
     each(0, chips, lambda d: pair_copy(d).wait_send())
+    each(1, 2 * chips, lambda d: wave_copy(d, lat).wait_send())
     each(1, members, lambda d: thin_copy(d).wait_send())
     each(1, members // 2, lambda e: wide_copy(e, z).wait_send())
     half_copy.wait_send()
 
 
-def all_inverse_roots(partial_gram, denominator, side):
-    chips = partial_gram.shape[0]
+def transformed(waves, table_parts, select, denominator, owned, side):
+    devices, per_device = waves.shape[:2]
+    chips = devices // 2
     members = lax.axis_size("mem")
     half = LEVELS // 2
     dma = pltpu.SemaphoreType.DMA
+    stride = (per_device + 7) // 8 * 8
+    counts = [devices, chips, chips, members, members // 2, 1, chips, chips]
     return pl.pallas_call(
         functools.partial(band_kernel, side, chips, members),
-        out_shape=jax.ShapeDtypeStruct((chips, LEVELS, LEVELS), jnp.float32),
-        in_specs=[pl.BlockSpec(memory_space=pltpu.VMEM)] * 2,
-        out_specs=pl.BlockSpec(memory_space=pltpu.VMEM),
+        out_shape=(
+            jax.ShapeDtypeStruct((2, owned, MM, LEVELS), jnp.bfloat16),
+            jax.ShapeDtypeStruct((chips, LEVELS, LEVELS), jnp.float32),
+        ),
+        in_specs=[pl.BlockSpec(memory_space=pltpu.VMEM)] * 8,
+        out_specs=(pl.BlockSpec(memory_space=pltpu.VMEM),) * 2,
         scratch_shapes=[
+            pltpu.VMEM((MM, *table_parts[1].shape), jnp.float32),
+            pltpu.VMEM(waves.shape, jnp.bfloat16),
+            pltpu.VMEM(((devices + 1) * stride, LEVELS), jnp.float32),
+            pltpu.VMEM((owned, chips * SLOTS, 2 * LEVELS), jnp.bfloat16),
+            pltpu.VMEM((owned, chips * SLOTS, 2 * LEVELS), jnp.bfloat16),
+            pltpu.VMEM((chips, LEVELS, LEVELS), jnp.float32),
             pltpu.VMEM((chips, half, LEVELS), jnp.float32),
             pltpu.VMEM((chips, half, LEVELS), jnp.float32),
             pltpu.VMEM((chips, half, LEVELS), jnp.float32),
             pltpu.VMEM((half, LEVELS), jnp.float32),
             pltpu.VMEM((members, 8, LEVELS), jnp.float32),
             pltpu.VMEM((LEVELS, LEVELS), jnp.float32),
-            dma((chips,)),
-            dma((chips,)),
-            dma((chips,)),
-            dma((chips,)),
-            dma((members,)),
-            dma((members,)),
-            dma((members // 2,)),
-            dma((members // 2,)),
-            dma((1,)),
-            dma((1,)),
-            dma((chips,)),
-            dma((chips,)),
-            dma((chips,)),
-            dma((chips,)),
-        ],
-        compiler_params=pltpu.CompilerParams(collective_id=0, has_side_effects=True),
-    )(partial_gram, denominator)
+        ]
+        + [dma((count,)) for count in counts for way in range(2)],
+        compiler_params=pltpu.CompilerParams(
+            collective_id=0, has_side_effects=True, vmem_limit_bytes=48 * 2**20
+        ),
+    )(waves, *table_parts, select, select.T, denominator)
 
 
 def body(perturbation, owner_map, band_widths):
-    members = perturbation.shape[0]
-    lat_rows = perturbation.shape[1]
+    members, lat_rows = perturbation.shape[:2]
     lat_devices = lax.axis_size("lat")
     lat_index = lax.axis_index("lat")
-    owned_count = MM // lat_devices
-    wave_table = fourier_table(owner_map, NLON)
+    owned = MM // lat_devices
+    wave_table = fourier_table(owner_map, NLON).reshape(2, lat_devices, owned, NLON)
     waves = jnp.einsum(
-        "rpk,ajkl->arpjl", wave_table, perturbation, preferred_element_type=jnp.float32
+        "rdqk,jkl->drqjl", wave_table, perturbation[0], preferred_element_type=jnp.float32
     ).astype(jnp.bfloat16)
-    owned_waves = lax.dynamic_slice_in_dim(owner_map, lat_index * owned_count, owned_count, 0)
-    poly_table = legendre_table(owned_waves.astype(jnp.float32), lat_rows * lat_devices)
-    spectral = jnp.einsum(
-        "qnj,arqjl->arqnl",
-        poly_table,
-        lax.all_to_all(waves, "lat", split_axis=2, concat_axis=3, tiled=True),
-        preferred_element_type=jnp.float32,
-    ).astype(jnp.bfloat16)
-    band_start, band_end, slot_rows, band_keep = band_rows(band_widths)
+    waves = waves.reshape(lat_devices, 2 * owned * lat_rows, LEVELS)
+    owned_waves = lax.dynamic_slice_in_dim(owner_map, lat_index * owned, owned, 0)
+    table_parts = legendre_start(
+        owned_waves.astype(jnp.float32), lat_rows * lat_devices, lat_rows
+    )
+    band_end = jnp.cumsum(band_widths)
+    band_start = band_end - band_widths
+    slot = jnp.arange(SLOTS, dtype=jnp.int32)[None, :]
+    slot_row = jnp.where(slot < band_widths[:, None], band_start[:, None] + slot, -1)
     row_index = jnp.arange(MM, dtype=jnp.int32)
-    selector = (row_index[:, None] == slot_rows.reshape(-1)[None, :]) & band_keep.reshape(-1)[
-        None, :
-    ]
-    select_low = selector.astype(jnp.bfloat16)
-    masked = jnp.einsum(
-        "arqnl,ns->arqsl", spectral, select_low, preferred_element_type=jnp.float32
-    ).astype(jnp.bfloat16)
-    masked = masked.reshape(members, 2, owned_count, BANDS, MOST, LEVELS)
-    partial_gram = jnp.einsum(
-        "arqbtk,arqbtl->bkl", masked, masked, preferred_element_type=jnp.float32
-    )
+    select = (slot_row.reshape(-1)[:, None] == row_index[None, :]).astype(jnp.bfloat16)
     member_total = members * lax.axis_size("mem")
-    bands_here = lax.axis_size("lat") // BANDS
-    band = lat_index // bands_here
+    band = lat_index // (lat_devices // BANDS)
     own_start = lax.dynamic_slice_in_dim(band_start, band, 1, 0)
     own_end = lax.dynamic_slice_in_dim(band_end, band, 1, 0)
     span = (own_end * own_end - own_start * own_start).astype(jnp.float32)
     denominator = jnp.broadcast_to((member_total - 1.0) * span[:, None], (1, LEVELS))
-    inverse_root = all_inverse_roots(partial_gram, denominator, CHIP_SIDE)
-    root_low = inverse_root.astype(jnp.bfloat16)
-    moved = jnp.einsum("arqbtk,blk->arqbtl", masked, root_low, preferred_element_type=jnp.float32)
-    moved = moved.astype(jnp.bfloat16).reshape(members, 2, owned_count, BANDS * MOST, LEVELS)
-    whitened = jnp.einsum(
-        "arqsl,ns->arqnl", moved, select_low, preferred_element_type=jnp.float32
+    whitened, inverse_root = transformed(
+        waves, table_parts, select, denominator, owned, CHIP_SIDE
     )
-    return (whitened.astype(jnp.bfloat16), inverse_root)
+    return (whitened[None], inverse_root)
 
 
 def solution(mesh):

time: 93.2 us -> 89.3 us (0.958)
  the two profiles are of different devices: /device:TPU:1 before, /device:TPU:7 now
where the time goes in v3:
time: 89.3 us; the launch traced here: 89 us
  Pallas kernels  76.8 us (86%)
  local copies, waits for them, and re-layouts  4.8 us (5%)
  other arithmetic  4.1 us (5%)
  between operations  2.74 us (3%)
    pallas_call x1, Pallas kernels, transformed(): pl.pallas_call(functools.partial(band_kernel, side, chips, members), out_...  76.8 us
    unnamed x18, local copies, waits for them, and re-layouts  2.95 us

profile of v3, /device:TPU:7, one launch (start us, length us, event | category | flops | bytes accessed | tf_op | source)
XLA Modules:
  0.0 89.0 jit_solution(17513197336138077009)
XLA Ops:
  0.6 0.0 copy-start
  0.7 0.9 dynamic-slice_convert_fusion
  1.6 0.2 select_reduce_fusion
  1.8 0.8 add_multiply_fusion
  2.5 0.1 broadcast_in_dim.26.zonal_ref
  2.6 0.1 add_exponential_fusion
  2.7 0.7 copy.16
  3.5 0.5 fusion.8
  4.0 0.1 reduce
  4.1 0.7 sub.10
  4.8 0.6 dynamic_slice.11
  7.3 0.7 add_select_fusion
  8.0 0.1 select_n.30
  8.2 0.6 copy-done.4
  8.8 0.3 fusion
  9.1 0.2 copy.14
  9.3 0.4 convolution_convert_fusion
  9.7 0.2 copy.17.waves_ref
  9.9 0.1 fusion.1.select_ref
  10.0 0.5 copy-done.1
  10.5 0.0 copy-done.2
  10.6 76.8 %shard_map.104 = (bf16[2,5,160,128]{3,2,1,0:T(8,128)(2,1)S(1)}, f32[16,128,128]{2,1,0:T(8,128)S(1)}) custom-call(bf16[32,50,128]{2,1,0:T(8,128)(2,1)S(1)} %copy.17.waves_ref, f32[8,128]{1,0:T(8,128)S(1)} %broadcast_in_dim.26.zonal_ref, f32[8,256]{1,0:T(8,128)S(1)} %pad.9.start_ref, f32[8,256]{1,0:T(8,128)S(1)} %copy-done.2, f32[8,256]{1,0:T(8,128)S(1)} %copy-done.1, ...), custom_call_target="tpu_custom_call" | custom-call | tf_op jit(solution)/shard_map/pallas_call | solution.py:448
  87.3 0.8 copy.26
  88.1 1.0 %copy.27 = f32[16,128,128]{2,1,0:T(8,128)} copy(f32[16,128,128]{2,1,0:T(8,128)S(1)} %get-tuple-element.9) | data formatting | bytes 2097152
  (17 shorter events, 0.1 us)
Async XLA Ops:
  0.6 8.6 %copy-start = (bf16[1,5,320,128]{3,2,1,0:T(8,128)(2,1)S(1)}, bf16[1,5,320,128]{3,2,1,0:T(8,128)(2,1)}, u32[]{:S(2)}) copy-start(bf16[1,5,320,128]{3,2,1,0:T(8,128)(2,1)} %param.9) | copy-start | bytes 1228804
  0.6 0.9 %copy-start.6 = (f32[160]{0:T(256)S(1)}, f32[160]{0:T(256)}, u32[]{:S(2)}) copy-start(f32[160]{0:T(256)} %constant.69) | copy-start | bytes 1924
  0.7 0.9 %copy-start.7 = (f32[160]{0:T(256)S(1)}, f32[160]{0:T(256)}, u32[]{:S(2)}) copy-start(f32[160]{0:T(256)} %constant.68) | copy-start | bytes 1924
  0.7 1.9 %copy-start.5 = (f32[160]{0:T(256)S(1)}, f32[160]{0:T(256)}, u32[]{:S(2)}) copy-start(f32[160]{0:T(256)} %constant.70) | copy-start | bytes 1924
  0.7 7.5 %copy-start.3 = (bf16[2,160,320]{2,1,0:T(8,128)(2,1)S(1)}, bf16[2,160,320]{2,1,0:T(8,128)(2,1)}, u32[]{:S(2)}) copy-start(bf16[2,160,320]{2,1,0:T(8,128)(2,1)} %constant.66) | copy-start | bytes 614404
  8.1 0.7 copy-start.4
  9.8 0.7 copy-start.1
  9.8 0.7 copy-start.2

commit v4 on v3

--- a/solution.py
+++ b/solution.py
@@ -20,8 +20,7 @@
 shrink_weight = 0.2
 
 
-def legendre_rows(zonal_ref, start_ref, cosine_ref, weight_ref, rows_ref):
-    zonal = zonal_ref[...]
+def legendre_rows(zonal, start_ref, cosine_ref, weight_ref, rows_ref):
     zonal_square = zonal * zonal
     lanes = start_ref.shape[1] // 128
     start = [start_ref[:, 128 * c : 128 * (c + 1)] for c in range(lanes)]
@@ -57,29 +56,57 @@
     lax.fori_loop(0, MM // 8, advance, (zero,) * (2 * lanes))
 
 
-def legendre_start(zonal_orders, lat_count, lat_rows):
-    owned = zonal_orders.shape[0]
-    rows, lanes = 8, (lat_count + 127) // 128 * 128
+def latitude_rows(lat_count, lat_rows):
+    rows, lanes = 8, (max(lat_count, MM) + 127) // 128 * 128
     devices = lat_count // lat_rows
     place = np.arange(lat_count)
     colatitude = np.pi * (place % devices * lat_rows + place // devices + 0.5) / lat_count
     counter = np.arange(1, MM + 1)
-    log_ratio = np.log((2.0 * counter - 1.0) / (2.0 * counter)).astype(np.float32)
-    log_sine = np.log(np.sin(colatitude)).astype(np.float32)
+    log_ratio = np.log((2.0 * counter - 1.0) / (2.0 * counter))
 
     def spread(row):
-        return np.tile(np.pad(row, (0, lanes - lat_count)).astype(np.float32), (rows, 1))
-
-    cosine = spread(np.cos(colatitude))
-    weight = spread(np.sqrt(np.pi / lat_count) * np.sin(colatitude))
-    log_factor = jnp.sum(
-        jnp.where(counter[None, :] <= zonal_orders[:, None], log_ratio[None, :], 0.0), axis=1
-    )
-    log_norm = 0.5 * jnp.log((2.0 * zonal_orders + 1.0) / 2.0) + 0.5 * log_factor
-    start = jnp.exp(log_norm[:, None] + zonal_orders[:, None] * log_sine[None, :])
-    start = jnp.pad(start, ((0, rows - owned), (0, lanes - lat_count)))
-    zonal = jnp.broadcast_to(jnp.pad(zonal_orders, (0, rows - owned))[:, None], (rows, 128))
-    return (zonal, start, cosine, weight)
+        return np.tile(np.pad(row, (0, lanes - row.size)).astype(np.float32), (rows, 1))
+
+    sine = np.sin(colatitude)
+    weight = np.sqrt(np.pi / lat_count) * sine
+    return (spread(log_ratio), spread(np.log(sine)), spread(np.cos(colatitude)), spread(weight))
+
+
+def owned_orders(owner, first):
+    rows, count = 8, owner.shape[1]
+    row = lax.broadcasted_iota(jnp.int32, (rows, count), 0)
+    place = lax.broadcasted_iota(jnp.int32, (rows, count), 1)
+    held = jnp.broadcast_to(owner.astype(jnp.float32), (rows, count))
+    return jnp.sum(jnp.where(place == first + row, held, 0.0), axis=1, keepdims=True)
+
+
+def first_values(orders, log_ratio, log_sine):
+    counter = lax.broadcasted_iota(jnp.int32, log_ratio.shape, 1).astype(jnp.float32) + 1.0
+    log_factor = jnp.sum(jnp.where(counter <= orders, log_ratio, 0.0), axis=1, keepdims=True)
+    log_norm = 0.5 * jnp.log((2.0 * orders + 1.0) / 2.0) + 0.5 * log_factor
+    return jnp.exp(log_norm + orders * log_sine)
+
+
+def slot_selectors(widths, bands, total):
+    slots, lanes = bands * SLOTS, widths.shape[1]
+    wide = widths.astype(jnp.float32)
+    band = lax.broadcasted_iota(jnp.int32, (slots, lanes), 0) // SLOTS
+    other = lax.broadcasted_iota(jnp.int32, (slots, lanes), 1)
+    rows = jnp.broadcast_to(wide, (slots, lanes))
+    start = jnp.sum(jnp.where(other < band, rows, 0.0), axis=1, keepdims=True)
+    width = jnp.sum(jnp.where(other == band, rows, 0.0), axis=1, keepdims=True)
+    place = (lax.broadcasted_iota(jnp.int32, (slots, 1), 0) % SLOTS).astype(jnp.float32)
+    degree = jnp.where(place < width, start + place, -1.0)
+    row = lax.broadcasted_iota(jnp.int32, (slots, total), 1).astype(jnp.float32)
+    return jnp.where(degree == row, 1.0, 0.0)
+
+
+def band_span(widths, band):
+    other = lax.broadcasted_iota(jnp.int32, widths.shape, 1)
+    wide = widths.astype(jnp.float32)
+    start = jnp.sum(jnp.where(other < band, wide, 0.0), axis=1, keepdims=True)
+    end = jnp.sum(jnp.where(other <= band, wide, 0.0), axis=1, keepdims=True)
+    return end * end - start * start
 
 
 def fourier_table(orders, lon_count):
@@ -127,16 +154,18 @@
     chips,
     members,
     waves_ref,
-    zonal_ref,
-    start_ref,
+    owner_ref,
+    widths_ref,
+    ratio_ref,
+    sine_ref,
     cosine_ref,
     weight_ref,
-    select_ref,
-    spread_ref,
-    denominator_ref,
     white_ref,
     out_ref,
     rows_ref,
+    start_ref,
+    select_ref,
+    spread_ref,
     arrived,
     grid,
     masked,
@@ -223,7 +252,13 @@
 
     each(1, members, lambda d: greet({"mem": z_after(d)}))
     each(1, 2 * chips, lambda d: greet({"lat": lat_after(d)}))
-    legendre_rows(zonal_ref, start_ref, cosine_ref, weight_ref, rows_ref)
+    orders = owned_orders(owner_ref[...], lat * masked.shape[0])
+    start_ref[...] = first_values(orders, ratio_ref[...], sine_ref[...])
+    zonal = jnp.broadcast_to(orders, (orders.shape[0], 128))
+    select = slot_selectors(widths_ref[...], chips, select_ref.shape[1])
+    select_ref[...] = select.astype(jnp.bfloat16)
+    spread_ref[...] = jnp.transpose(select).astype(jnp.bfloat16)
+    legendre_rows(zonal, start_ref, cosine_ref, weight_ref, rows_ref)
     pl.semaphore_wait(barrier, members - 1 + 2 * chips - 1)
 
     def wave_copy(d, source):
@@ -255,7 +290,7 @@
         both = jnp.concatenate([field(0, q), field(1, q)], axis=1).astype(jnp.bfloat16)
         coefficients = jnp.dot(table, both, preferred_element_type=jnp.float32)
         masked[q] = jnp.dot(
-            select_ref[...],
+            select_ref[:, :MM],
             coefficients.astype(jnp.bfloat16),
             preferred_element_type=jnp.float32,
         ).astype(jnp.bfloat16)
@@ -316,15 +351,21 @@
         add_up(chip_after(d))
         pair_copy(d).start()
 
-    each(1, chips, begin)
-    begin(0)
 
     def forward(d):
         pair_copy(d).wait_recv()
         summed[d] = gram_ref[chip_after(d), rows, :] + pair[d]
         lat_copy(d).start()
 
-    each(1, chips, forward)
+    def begin_and_forward(d):
+        begin(d)
+        forward(d - lag)
+
+    lag = min(3, chips - 1)
+    each(1, 1 + lag, begin)
+    each(1 + lag, chips, begin_and_forward)
+    begin(0)
+    each(chips - lag, chips, forward)
     pair_copy(0).wait_recv()
     own = gram_ref[chip, rows, :] + pair[0]
 
@@ -378,7 +419,7 @@
     half_copy.start()
     half_arrival.wait_recv()
 
-    out_ref[chip] = inverse_root_of(full[...], denominator_ref[...])
+    out_ref[chip] = inverse_root_of(full[...], (members - 1.0) * band_span(widths_ref[...], chip))
 
     def root_copy(d, owner):
         return send(
@@ -419,7 +460,7 @@
     take_over(chips - 1)
     for q in range(owned):
         result = jnp.dot(
-            spread_ref[...], moved[q], preferred_element_type=jnp.float32
+            spread_ref[:MM], moved[q], preferred_element_type=jnp.float32
         ).astype(jnp.bfloat16)
         for r in range(2):
             white_ref[r, q] = result[:, LEVELS * r : LEVELS * (r + 1)]
@@ -437,12 +478,13 @@
     half_copy.wait_send()
 
 
-def transformed(waves, table_parts, select, denominator, owned, side):
+def transformed(waves, owner_map, band_widths, latitudes, owned, side):
     devices, per_device = waves.shape[:2]
     chips = devices // 2
     members = lax.axis_size("mem")
     half = LEVELS // 2
     dma = pltpu.SemaphoreType.DMA
+    lanes = (MM + 127) // 128 * 128
     stride = (per_device + 7) // 8 * 8
     counts = [devices, chips, chips, members, members // 2, 1, chips, chips]
     return pl.pallas_call(
@@ -451,10 +493,13 @@
             jax.ShapeDtypeStruct((2, owned, MM, LEVELS), jnp.bfloat16),
             jax.ShapeDtypeStruct((chips, LEVELS, LEVELS), jnp.float32),
         ),
-        in_specs=[pl.BlockSpec(memory_space=pltpu.VMEM)] * 8,
+        in_specs=[pl.BlockSpec(memory_space=pltpu.VMEM)] * 7,
         out_specs=(pl.BlockSpec(memory_space=pltpu.VMEM),) * 2,
         scratch_shapes=[
-            pltpu.VMEM((MM, *table_parts[1].shape), jnp.float32),
+            pltpu.VMEM((MM, *latitudes[0].shape), jnp.float32),
+            pltpu.VMEM(latitudes[0].shape, jnp.float32),
+            pltpu.VMEM((chips * SLOTS, lanes), jnp.bfloat16),
+            pltpu.VMEM((lanes, chips * SLOTS), jnp.bfloat16),
             pltpu.VMEM(waves.shape, jnp.bfloat16),
             pltpu.VMEM(((devices + 1) * stride, LEVELS), jnp.float32),
             pltpu.VMEM((owned, chips * SLOTS, 2 * LEVELS), jnp.bfloat16),
@@ -471,37 +516,21 @@
         compiler_params=pltpu.CompilerParams(
             collective_id=0, has_side_effects=True, vmem_limit_bytes=48 * 2**20
         ),
-    )(waves, *table_parts, select, select.T, denominator)
+    )(waves, owner_map[None], band_widths[None], *latitudes)
 
 
 def body(perturbation, owner_map, band_widths):
-    members, lat_rows = perturbation.shape[:2]
+    lat_rows = perturbation.shape[1]
     lat_devices = lax.axis_size("lat")
-    lat_index = lax.axis_index("lat")
     owned = MM // lat_devices
     wave_table = fourier_table(owner_map, NLON).reshape(2, lat_devices, owned, NLON)
     waves = jnp.einsum(
         "rdqk,jkl->drqjl", wave_table, perturbation[0], preferred_element_type=jnp.float32
     ).astype(jnp.bfloat16)
     waves = waves.reshape(lat_devices, 2 * owned * lat_rows, LEVELS)
-    owned_waves = lax.dynamic_slice_in_dim(owner_map, lat_index * owned, owned, 0)
-    table_parts = legendre_start(
-        owned_waves.astype(jnp.float32), lat_rows * lat_devices, lat_rows
-    )
-    band_end = jnp.cumsum(band_widths)
-    band_start = band_end - band_widths
-    slot = jnp.arange(SLOTS, dtype=jnp.int32)[None, :]
-    slot_row = jnp.where(slot < band_widths[:, None], band_start[:, None] + slot, -1)
-    row_index = jnp.arange(MM, dtype=jnp.int32)
-    select = (slot_row.reshape(-1)[:, None] == row_index[None, :]).astype(jnp.bfloat16)
-    member_total = members * lax.axis_size("mem")
-    band = lat_index // (lat_devices // BANDS)
-    own_start = lax.dynamic_slice_in_dim(band_start, band, 1, 0)
-    own_end = lax.dynamic_slice_in_dim(band_end, band, 1, 0)
-    span = (own_end * own_end - own_start * own_start).astype(jnp.float32)
-    denominator = jnp.broadcast_to((member_total - 1.0) * span[:, None], (1, LEVELS))
+    latitudes = latitude_rows(lat_rows * lat_devices, lat_rows)
     whitened, inverse_root = transformed(
-        waves, table_parts, select, denominator, owned, CHIP_SIDE
+        waves, owner_map, band_widths, latitudes, owned, CHIP_SIDE
     )
     return (whitened[None], inverse_root)
 

time: 89.3 us -> 83.8 us (0.938)
  other arithmetic: 4.1 us -> 0 us
  between operations: 2.74 us -> 0.74 us
  local copies, waits for them, and re-layouts: 4.8 us -> 3.35 us
  Pallas kernels: 76.8 us -> 78 us
  matrix products: 0.65 us -> 1.59 us
    pallas_call x1, Pallas kernels: 76.8 us -> 78 us  [transformed(): pl.pallas_call(functools.partial(band_kernel, side, chips, members), out_...]
    convert_element_type x3 -> x0, other arithmetic: 1.03 us -> none  [the longest x1 0.86 us: body(): owned_waves.astype(jnp.float32)]
    dot_general x1, matrix products: 0.27 us -> 1.21 us  [fourier_table(): jnp.einsum('pm,rmk->rpk', pick, waves, preferred_element_type=jnp.float32)]
    unnamed x18 -> x16, local copies, waits for them, and re-layouts: 2.95 us -> 2.99 us
where the time goes in v4:
time: 83.8 us; the launch traced here: 83.6 us
  Pallas kernels  78 us (93%)
  local copies, waits for them, and re-layouts  3.35 us (4%)
  matrix products  1.59 us (2%)
    pallas_call x1, Pallas kernels, transformed(): pl.pallas_call(functools.partial(band_kernel, side, chips, members), out_...  78 us
    unnamed x16, local copies, waits for them, and re-layouts  2.99 us

profile of v4, /device:TPU:7, one launch (start us, length us, event | category | flops | bytes accessed | tf_op | source)
XLA Modules:
  0.0 83.6 jit_solution(6273658633587456484)
XLA Ops:
  0.6 0.0 copy-start
  0.6 0.0 copy-start.5
  0.7 0.7 copy-done.5
  1.4 1.2 %fusion = bf16[2,160,320]{2,1,0:T(8,128)(2,1)S(1)} fusion(bf16[2,160,320]{2,1,0:T(8,128)(2,1)} %constant.16, s32[160]{0:T(256)S(1)} %copy-done.5), kind=kOutput, calls=%fused_computation.2 | convolution fusion | flops 32896000 | bytes 410240 | tf_op jit(solution)/shard_map/pm,rmk->rpk/dot_general | solution.py:119
  2.6 0.2 copy.12
  2.8 0.0 copy-done
  2.8 0.4 convolution_convert_fusion
  3.2 0.0 copy-start.1
  3.2 0.0 copy-start.2
  3.2 0.0 copy-start.3
  3.2 0.0 copy-start.4
  3.2 0.0 copy-start.6
  3.2 0.2 copy.14.waves_ref
  3.4 0.5 copy-done.1
  3.9 0.0 copy-done.2
  3.9 0.0 copy-done.3
  3.9 0.0 copy-done.4
  3.9 0.0 copy-done.6
  3.9 78.0 %shard_map.95 = (bf16[2,5,160,128]{3,2,1,0:T(8,128)(2,1)S(1)}, f32[16,128,128]{2,1,0:T(8,128)S(1)}) custom-call(bf16[32,50,128]{2,1,0:T(8,128)(2,1)S(1)} %copy.14.waves_ref, s32[1,160]{1,0:T(1,128)S(1)} %bitcast.23, s32[1,16]{1,0:T(1,128)S(1)} %bitcast.24, f32[8,256]{1,0:T(8,128)S(1)} %copy-done.4, f32[8,256]{1,0:T(8,128)S(1)} %copy-done.3, ...), custom_call_target="tpu_custom_call" | custom-call | tf_op jit(solution)/shard_map/pallas_call | solution.py:490
  81.9 0.8 copy.23
  82.7 1.0 %copy.24 = f32[16,128,128]{2,1,0:T(8,128)} copy(f32[16,128,128]{2,1,0:T(8,128)S(1)} %get-tuple-element.9) | data formatting | bytes 2097152
Async XLA Ops:
  0.6 2.2 %copy-start = (bf16[1,5,320,128]{3,2,1,0:T(8,128)(2,1)S(1)}, bf16[1,5,320,128]{3,2,1,0:T(8,128)(2,1)}, u32[]{:S(2)}) copy-start(bf16[1,5,320,128]{3,2,1,0:T(8,128)(2,1)} %param.8) | copy-start | bytes 1228804
  0.6 0.7 copy-start.5
  3.2 0.7 copy-start.1
  3.2 0.7 copy-start.2
  3.2 0.7 copy-start.3
  3.2 0.7 copy-start.4
  3.2 0.7 copy-start.6

commit v5 on v4

--- a/solution.py
+++ b/solution.py
@@ -129,9 +129,20 @@
     def whole_sum(array):
         return jnp.sum(jnp.sum(array, axis=0, keepdims=True), axis=1, keepdims=True)
 
+    def pieces(array):
+        first = array.astype(jnp.bfloat16)
+        rest = array - first.astype(jnp.float32)
+        second = rest.astype(jnp.bfloat16)
+        third = (rest - second.astype(jnp.float32)).astype(jnp.bfloat16)
+        return (first, second, third)
+
     def product(left, right):
-        return lax.dot(
-            left, right, precision=lax.Precision.HIGHEST, preferred_element_type=jnp.float32
+        a, b = pieces(left), pieces(right)
+        terms = ((0, 2), (1, 1), (2, 0), (0, 1), (1, 0), (0, 0))
+        return jnp.dot(
+            jnp.concatenate([a[i] for i, j in terms], axis=1),
+            jnp.concatenate([b[j] for i, j in terms], axis=0),
+            preferred_element_type=jnp.float32,
         )
 
     covariance = gram / denominator

time: 83.8 us -> 83.7 us (level)
  no operation moved by 1% of the time
where the time goes in v5:
time: 83.7 us; the launch traced here: 83.5 us
  Pallas kernels  77.8 us (93%)
  local copies, waits for them, and re-layouts  3.35 us (4%)
  matrix products  1.59 us (2%)
    pallas_call x1, Pallas kernels, transformed(): pl.pallas_call(functools.partial(band_kernel, side, chips, members), out_...  77.8 us
    unnamed x16, local copies, waits for them, and re-layouts  2.99 us

profile of v5, /device:TPU:7, one launch (start us, length us, event | category | flops | bytes accessed | tf_op | source)
XLA Modules:
  0.0 83.5 jit_solution(3124962998332694791)
XLA Ops:
  0.6 0.0 copy-start
  0.6 0.0 copy-start.5
  0.7 0.7 copy-done.5
  1.4 1.2 %fusion = bf16[2,160,320]{2,1,0:T(8,128)(2,1)S(1)} fusion(bf16[2,160,320]{2,1,0:T(8,128)(2,1)} %constant.16, s32[160]{0:T(256)S(1)} %copy-done.5), kind=kOutput, calls=%fused_computation.2 | convolution fusion | flops 32896000 | bytes 410240 | tf_op jit(solution)/shard_map/pm,rmk->rpk/dot_general | solution.py:119
  2.6 0.2 copy.12
  2.8 0.0 copy-done
  2.8 0.4 convolution_convert_fusion
  3.2 0.0 copy-start.1
  3.2 0.0 copy-start.2
  3.2 0.0 copy-start.3
  3.2 0.0 copy-start.4
  3.2 0.0 copy-start.6
  3.2 0.2 copy.14.waves_ref
  3.4 0.5 copy-done.1
  3.9 0.0 copy-done.2
  3.9 0.0 copy-done.3
  3.9 0.0 copy-done.4
  3.9 0.0 copy-done.6
  3.9 77.8 %shard_map.95 = (bf16[2,5,160,128]{3,2,1,0:T(8,128)(2,1)S(1)}, f32[16,128,128]{2,1,0:T(8,128)S(1)}) custom-call(bf16[32,50,128]{2,1,0:T(8,128)(2,1)S(1)} %copy.14.waves_ref, s32[1,160]{1,0:T(1,128)S(1)} %bitcast.23, s32[1,16]{1,0:T(1,128)S(1)} %bitcast.24, f32[8,256]{1,0:T(8,128)S(1)} %copy-done.4, f32[8,256]{1,0:T(8,128)S(1)} %copy-done.3, ...), custom_call_target="tpu_custom_call" | custom-call | tf_op jit(solution)/shard_map/pallas_call | solution.py:501
  81.8 0.8 copy.23
  82.5 1.0 %copy.24 = f32[16,128,128]{2,1,0:T(8,128)} copy(f32[16,128,128]{2,1,0:T(8,128)S(1)} %get-tuple-element.9) | data formatting | bytes 2097152
Async XLA Ops:
  0.6 2.2 %copy-start = (bf16[1,5,320,128]{3,2,1,0:T(8,128)(2,1)S(1)}, bf16[1,5,320,128]{3,2,1,0:T(8,128)(2,1)}, u32[]{:S(2)}) copy-start(bf16[1,5,320,128]{3,2,1,0:T(8,128)(2,1)} %param.8) | copy-start | bytes 1228804
  0.6 0.7 copy-start.5
  3.2 0.7 copy-start.1
  3.2 0.7 copy-start.2
  3.2 0.7 copy-start.3
  3.2 0.7 copy-start.4
  3.2 0.7 copy-start.6

commit v6 on v5

--- a/solution.py
+++ b/solution.py
@@ -269,7 +269,6 @@
     select = slot_selectors(widths_ref[...], chips, select_ref.shape[1])
     select_ref[...] = select.astype(jnp.bfloat16)
     spread_ref[...] = jnp.transpose(select).astype(jnp.bfloat16)
-    legendre_rows(zonal, start_ref, cosine_ref, weight_ref, rows_ref)
     pl.semaphore_wait(barrier, members - 1 + 2 * chips - 1)
 
     def wave_copy(d, source):
@@ -283,6 +282,7 @@
 
     each(1, 2 * chips, lambda d: wave_copy(d, lat).start())
     arrived[lat] = waves_ref[lat]
+    legendre_rows(zonal, start_ref, cosine_ref, weight_ref, rows_ref)
     each(1, 2 * chips, lambda d: wave_copy(d, lat_before(d)).wait_recv())
     devices, per_device = arrived.shape[0], arrived.shape[1]
     owned = masked.shape[0]

time: 83.7 us -> 83.7 us (level)
  no operation moved by 1% of the time
where the time goes in v6:
time: 83.7 us; the launch traced here: 83.5 us
  Pallas kernels  77.8 us (93%)
  local copies, waits for them, and re-layouts  3.35 us (4%)
  matrix products  1.59 us (2%)
    pallas_call x1, Pallas kernels, transformed(): pl.pallas_call(functools.partial(band_kernel, side, chips, members), out_...  77.8 us
    unnamed x16, local copies, waits for them, and re-layouts  2.99 us

profile of v6, /device:TPU:7, one launch (start us, length us, event | category | flops | bytes accessed | tf_op | source)
XLA Modules:
  0.0 83.5 jit_solution(8855619279109165996)
XLA Ops:
  0.6 0.0 copy-start
  0.6 0.0 copy-start.5
  0.7 0.7 copy-done.5
  1.4 1.2 %fusion = bf16[2,160,320]{2,1,0:T(8,128)(2,1)S(1)} fusion(bf16[2,160,320]{2,1,0:T(8,128)(2,1)} %constant.16, s32[160]{0:T(256)S(1)} %copy-done.5), kind=kOutput, calls=%fused_computation.2 | convolution fusion | flops 32896000 | bytes 410240 | tf_op jit(solution)/shard_map/pm,rmk->rpk/dot_general | solution.py:119
  2.6 0.2 copy.12
  2.8 0.0 copy-done
  2.8 0.4 convolution_convert_fusion
  3.2 0.0 copy-start.1
  3.2 0.0 copy-start.2
  3.2 0.0 copy-start.3
  3.2 0.0 copy-start.4
  3.2 0.0 copy-start.6
  3.2 0.2 copy.14.waves_ref
  3.4 0.5 copy-done.1
  3.9 0.0 copy-done.2
  3.9 0.0 copy-done.3
  3.9 0.0 copy-done.4
  3.9 0.0 copy-done.6
  3.9 77.8 %shard_map.95 = (bf16[2,5,160,128]{3,2,1,0:T(8,128)(2,1)S(1)}, f32[16,128,128]{2,1,0:T(8,128)S(1)}) custom-call(bf16[32,50,128]{2,1,0:T(8,128)(2,1)S(1)} %copy.14.waves_ref, s32[1,160]{1,0:T(1,128)S(1)} %bitcast.23, s32[1,16]{1,0:T(1,128)S(1)} %bitcast.24, f32[8,256]{1,0:T(8,128)S(1)} %copy-done.4, f32[8,256]{1,0:T(8,128)S(1)} %copy-done.3, ...), custom_call_target="tpu_custom_call" | custom-call | tf_op jit(solution)/shard_map/pallas_call | solution.py:501
  81.7 0.8 copy.23
  82.5 1.0 %copy.24 = f32[16,128,128]{2,1,0:T(8,128)} copy(f32[16,128,128]{2,1,0:T(8,128)S(1)} %get-tuple-element.9) | data formatting | bytes 2097152
Async XLA Ops:
  0.6 2.2 %copy-start = (bf16[1,5,320,128]{3,2,1,0:T(8,128)(2,1)S(1)}, bf16[1,5,320,128]{3,2,1,0:T(8,128)(2,1)}, u32[]{:S(2)}) copy-start(bf16[1,5,320,128]{3,2,1,0:T(8,128)(2,1)} %param.8) | copy-start | bytes 1228804
  0.6 0.7 copy-start.5
  3.2 0.7 copy-start.1
  3.2 0.7 copy-start.2
  3.2 0.7 copy-start.3
  3.2 0.7 copy-start.4
  3.2 0.7 copy-start.6
